TPU v7x, 32 devices: a whole 2x2x4 slice. The times are simulated.
32 devices in a mesh: fsdp: 8 (over y, x, core), tensor: 4 (over z).
Axes of the slice: x: 2, y: 2, z: 4, core: 2. Of those that a mesh axis runs over, the one named last changes fastest.
Arguments:
- tokens: bfloat16 [16384, 768], P(('fsdp', 'tensor')), may hold values from -6 to 6
- cotangent: bfloat16 [16384, 768], P(('fsdp', 'tensor')), may hold values from -6 to 6
- w_query: bfloat16 [768, 768], P('fsdp', 'tensor'), may hold values from -0.21875 to 0.21875
- w_key: bfloat16 [768, 768], P('fsdp', 'tensor'), may hold values from -0.21875 to 0.21875
- w_value: bfloat16 [768, 768], P('fsdp', 'tensor'), may hold values from -0.21875 to 0.21875
- w_out: bfloat16 [768, 768], P('tensor', 'fsdp'), may hold values from -6 to 6
- w_up: bfloat16 [768, 3072], P('fsdp', 'tensor'), may hold values from -0.21875 to 0.21875
- w_down: bfloat16 [3072, 768], P('tensor', 'fsdp'), may hold values from -0.109375 to 0.109375
- b_query: bfloat16 [768], P(('tensor', 'fsdp')), may hold values from -3 to 3
- b_value: bfloat16 [768], P(('tensor', 'fsdp')), may hold values from -0.1875 to 0.1875
- b_up: bfloat16 [3072], P(('tensor', 'fsdp')), may hold values from -3 to 3
- b_out: bfloat16 [768], P('fsdp'), may hold values from -1.25 to 1.25
- b_down: bfloat16 [768], P('fsdp'), may hold values from -1.25 to 1.25
- gain_attn: bfloat16 [768], P('fsdp'), may hold values from 0.5 to 1.5
- shift_attn: bfloat16 [768], P('fsdp'), may hold values from -1.25 to 1.25
- gain_ffn: bfloat16 [768], P('fsdp'), may hold values from 0.5 to 1.5
- shift_ffn: bfloat16 [768], P('fsdp'), may hold values from -1.25 to 1.25
Outputs:
- output: float32 [16384, 768], P(('fsdp', 'tensor'))
- grad_tokens: float32 [16384, 768], P(('fsdp', 'tensor'))
- grad_w_query: float32 [768, 768], P('fsdp', 'tensor')
- grad_w_key: float32 [768, 768], P('fsdp', 'tensor')
- grad_w_value: float32 [768, 768], P('fsdp', 'tensor')
- grad_w_out: float32 [768, 768], P('tensor', 'fsdp')
- grad_w_up: float32 [768, 3072], P('fsdp', 'tensor')
- grad_w_down: float32 [3072, 768], P('tensor', 'fsdp')
- grad_b_query: float32 [768], P(('tensor', 'fsdp'))
- grad_b_value: float32 [768], P(('tensor', 'fsdp'))
- grad_b_up: float32 [3072], P(('tensor', 'fsdp'))
- grad_b_out: float32 [768], P('fsdp')
- grad_b_down: float32 [768], P('fsdp')
- grad_gain_attn: float32 [768], P('fsdp')
- grad_shift_attn: float32 [768], P('fsdp')
- grad_gain_ffn: float32 [768], P('fsdp')
- grad_shift_ffn: float32 [768], P('fsdp')
All inputs are finite; a program needn't handle non-finite values.
Results may differ from a plain program's by a relative error of at most 0.02.
Values may be sent and summed in bfloat16 or wider, within the bound.
A program may use at most 128 MiB of HBM per device.

v0:
```python
import jax
import jax.numpy as jnp
from jax import lax
from jax.sharding import PartitionSpec as P

HEAD = 64


EPSILON = 1e-12
CONTRACT_LAST = (((1,), (1,)), ((), ()))
CONTRACT_FIRST = (((0,), (0,)), ((), ()))


def normalize(values, gain, shift):
    average = jnp.mean(values, -1, keepdims=True)
    centered = values - average
    inverse = lax.rsqrt(jnp.mean(centered * centered, -1, keepdims=True) + EPSILON)
    return centered * inverse * gain + shift


def exact_gelu(values):
    return jax.nn.gelu(values, approximate=False)


def outer_sum(left, right):
    return lax.dot_general(left, right, CONTRACT_FIRST, preferred_element_type=jnp.float32)


def times_transposed(left, right):
    return lax.dot_general(left, right, CONTRACT_LAST, preferred_element_type=jnp.float32)


def local(
    tokens,
    cotangent,
    w_query,
    w_key,
    w_value,
    w_out,
    w_up,
    w_down,
    b_query,
    b_value,
    b_up,
    b_out,
    b_down,
    gain_attn,
    shift_attn,
    gain_ffn,
    shift_ffn,
):
    gathered = (
        lax.all_gather(w_query, "fsdp", axis=0, tiled=True),
        lax.all_gather(w_key, "fsdp", axis=0, tiled=True),
        lax.all_gather(w_value, "fsdp", axis=0, tiled=True),
        lax.all_gather(w_out, "fsdp", axis=1, tiled=True),
        lax.all_gather(w_up, "fsdp", axis=0, tiled=True),
        lax.all_gather(w_down, "fsdp", axis=1, tiled=True),
        lax.all_gather(b_query, "fsdp", axis=0, tiled=True),
        lax.all_gather(b_value, "fsdp", axis=0, tiled=True),
        lax.all_gather(b_up, "fsdp", axis=0, tiled=True),
        lax.all_gather(b_out, "fsdp", axis=0, tiled=True),
        lax.all_gather(b_down, "fsdp", axis=0, tiled=True),
        lax.all_gather(gain_attn, "fsdp", axis=0, tiled=True),
        lax.all_gather(shift_attn, "fsdp", axis=0, tiled=True),
        lax.all_gather(gain_ffn, "fsdp", axis=0, tiled=True),
        lax.all_gather(shift_ffn, "fsdp", axis=0, tiled=True),
    )
    (
        query_weight,
        key_weight,
        value_weight,
        out_weight,
        up_weight,
        down_weight,
        query_bias,
        value_bias,
        up_bias,
        out_bias,
        down_bias,
        attn_gain,
        attn_shift,
        ffn_gain,
        ffn_shift,
    ) = gathered
    own_rows = tokens.shape[0]
    seq_len = own_rows * lax.axis_size("tensor")
    heads = query_weight.shape[1] // HEAD
    span = min(512, seq_len)
    blocks = seq_len // span
    scale = HEAD ** (-0.5)
    full_tokens = lax.all_gather(tokens, "tensor", axis=0, tiled=True)
    query = (
        jnp.dot(full_tokens, query_weight, preferred_element_type=jnp.float32)
        + query_bias.astype(jnp.float32)
    ).astype(jnp.bfloat16)
    keys = jnp.dot(full_tokens, key_weight, preferred_element_type=jnp.float32).astype(jnp.bfloat16)
    values = (
        jnp.dot(full_tokens, value_weight, preferred_element_type=jnp.float32)
        + value_bias.astype(jnp.float32)
    ).astype(jnp.bfloat16)
    query_blocks = query.reshape(blocks, span, heads, HEAD)
    key_heads = keys.reshape(seq_len, heads, HEAD)
    value_heads = values.reshape(seq_len, heads, HEAD)

    def scores_of(piece):
        return (
            jnp.einsum("qhd,khd->hqk", piece, key_heads, preferred_element_type=jnp.float32) * scale
        )

    def forward_block(piece):
        scores = scores_of(piece)
        largest = jnp.max(scores, -1, keepdims=True)
        exponent = jnp.exp(scores - largest)
        total = jnp.sum(exponent, -1, keepdims=True)
        soft_low = (exponent / total).astype(jnp.bfloat16)
        result = jnp.einsum(
            "hqk,khd->qhd", soft_low, value_heads, preferred_element_type=jnp.float32
        )
        return (result.astype(jnp.bfloat16), largest, total)

    attended, largest_all, total_all = lax.map(forward_block, query_blocks)
    attended = attended.reshape(seq_len, heads * HEAD)
    attn_part = lax.psum_scatter(
        jnp.dot(attended, out_weight, preferred_element_type=jnp.float32).astype(jnp.bfloat16),
        "tensor",
        scatter_dimension=0,
        tiled=True,
    ).astype(jnp.float32)
    resid_attn = tokens.astype(jnp.float32) + (attn_part + out_bias.astype(jnp.float32))
    hidden, attn_norm_back = jax.vjp(
        normalize, resid_attn, attn_gain.astype(jnp.float32), attn_shift.astype(jnp.float32)
    )
    full_hidden = lax.all_gather(hidden.astype(jnp.bfloat16), "tensor", axis=0, tiled=True)
    pre_act = jnp.dot(full_hidden, up_weight, preferred_element_type=jnp.float32) + up_bias.astype(
        jnp.float32
    )
    activ, gelu_back = jax.vjp(exact_gelu, pre_act)
    activ_low = activ.astype(jnp.bfloat16)
    ffn_part = lax.psum_scatter(
        jnp.dot(activ_low, down_weight, preferred_element_type=jnp.float32).astype(jnp.bfloat16),
        "tensor",
        scatter_dimension=0,
        tiled=True,
    ).astype(jnp.float32)
    resid_ffn = hidden + (ffn_part + down_bias.astype(jnp.float32))
    output, ffn_norm_back = jax.vjp(
        normalize, resid_ffn, ffn_gain.astype(jnp.float32), ffn_shift.astype(jnp.float32)
    )
    matrices = (
        lax.all_gather(w_query, "fsdp", axis=0, tiled=True),
        lax.all_gather(w_key, "fsdp", axis=0, tiled=True),
        lax.all_gather(w_value, "fsdp", axis=0, tiled=True),
        lax.all_gather(w_out, "fsdp", axis=1, tiled=True),
        lax.all_gather(w_up, "fsdp", axis=0, tiled=True),
        lax.all_gather(w_down, "fsdp", axis=1, tiled=True),
    )
    back_query, back_key, back_value, back_out, back_up, back_down = matrices
    grad_resid_ffn, grad_gain_ffn, grad_shift_ffn = ffn_norm_back(cotangent.astype(jnp.float32))
    grad_ffn_full = lax.all_gather(
        grad_resid_ffn.astype(jnp.bfloat16), "tensor", axis=0, tiled=True
    )
    grad_down_bias = jnp.sum(grad_ffn_full, 0, dtype=jnp.float32)
    grad_down_weight = outer_sum(activ_low, grad_ffn_full)
    grad_activ = times_transposed(grad_ffn_full, back_down)
    grad_pre = gelu_back(grad_activ)[0].astype(jnp.bfloat16)
    grad_up_bias = jnp.sum(grad_pre, 0, dtype=jnp.float32)
    grad_up_weight = outer_sum(full_hidden, grad_pre)
    grad_hidden = grad_resid_ffn + lax.psum_scatter(
        times_transposed(grad_pre, back_up).astype(jnp.bfloat16),
        "tensor",
        scatter_dimension=0,
        tiled=True,
    ).astype(jnp.float32)
    grad_resid_attn, grad_gain_attn, grad_shift_attn = attn_norm_back(grad_hidden)
    grad_attn_full = lax.all_gather(
        grad_resid_attn.astype(jnp.bfloat16), "tensor", axis=0, tiled=True
    )
    grad_out_bias = jnp.sum(grad_attn_full, 0, dtype=jnp.float32)
    grad_out_weight = outer_sum(attended, grad_attn_full)
    grad_attended = times_transposed(grad_attn_full, back_out).astype(jnp.bfloat16)
    grad_blocks = grad_attended.reshape(blocks, span, heads, HEAD)

    def backward_block(carry, item):
        piece, grad_piece, largest, total = item
        soft = jnp.exp(scores_of(piece) - largest) / total
        soft_low = soft.astype(jnp.bfloat16)
        grad_soft = jnp.einsum(
            "qhd,khd->hqk", grad_piece, value_heads, preferred_element_type=jnp.float32
        )
        inner = jnp.sum(soft * grad_soft, -1, keepdims=True)
        grad_scores = (soft * (grad_soft - inner)).astype(jnp.bfloat16)
        grad_query_block = (
            jnp.einsum("hqk,khd->qhd", grad_scores, key_heads, preferred_element_type=jnp.float32)
            * scale
        )
        grad_key_sum = (
            carry[0]
            + jnp.einsum("hqk,qhd->khd", grad_scores, piece, preferred_element_type=jnp.float32)
            * scale
        )
        grad_value_sum = carry[1] + jnp.einsum(
            "hqk,qhd->khd", soft_low, grad_piece, preferred_element_type=jnp.float32
        )
        return ((grad_key_sum, grad_value_sum), grad_query_block.astype(jnp.bfloat16))

    zeros = jnp.zeros((seq_len, heads, HEAD), jnp.float32)
    (grad_key_sum, grad_value_sum), grad_query = lax.scan(
        backward_block, (zeros, zeros), (query_blocks, grad_blocks, largest_all, total_all)
    )
    grad_query = grad_query.reshape(seq_len, heads * HEAD)
    grad_keys = grad_key_sum.reshape(seq_len, heads * HEAD).astype(jnp.bfloat16)
    grad_values = grad_value_sum.reshape(seq_len, heads * HEAD).astype(jnp.bfloat16)
    grad_query_bias = jnp.sum(grad_query, 0, dtype=jnp.float32)
    grad_value_bias = jnp.sum(grad_values, 0, dtype=jnp.float32)
    grad_query_weight = outer_sum(full_tokens, grad_query)
    grad_key_weight = outer_sum(full_tokens, grad_keys)
    grad_value_weight = outer_sum(full_tokens, grad_values)
    token_terms = (
        times_transposed(grad_query, back_query)
        + times_transposed(grad_keys, back_key)
        + times_transposed(grad_values, back_value)
    )
    norm_terms = jnp.tile(
        jnp.stack([grad_gain_attn, grad_shift_attn, grad_gain_ffn, grad_shift_ffn]),
        (lax.axis_size("tensor"), 1),
    )
    token_part, norm_sums = (
        lax.psum_scatter(
            token_terms.astype(jnp.bfloat16), "tensor", scatter_dimension=0, tiled=True
        ).astype(jnp.float32),
        lax.psum_scatter(
            norm_terms.astype(jnp.bfloat16), "tensor", scatter_dimension=0, tiled=True
        ).astype(jnp.float32),
    )
    grad_tokens = grad_resid_attn + token_part
    shards = (
        lax.psum_scatter(grad_query_weight, "fsdp", scatter_dimension=0, tiled=True),
        lax.psum_scatter(grad_key_weight, "fsdp", scatter_dimension=0, tiled=True),
        lax.psum_scatter(grad_value_weight, "fsdp", scatter_dimension=0, tiled=True),
        lax.psum_scatter(grad_out_weight, "fsdp", scatter_dimension=1, tiled=True),
        lax.psum_scatter(grad_up_weight, "fsdp", scatter_dimension=0, tiled=True),
        lax.psum_scatter(grad_down_weight, "fsdp", scatter_dimension=1, tiled=True),
        lax.psum_scatter(grad_query_bias, "fsdp", scatter_dimension=0, tiled=True),
        lax.psum_scatter(grad_value_bias, "fsdp", scatter_dimension=0, tiled=True),
        lax.psum_scatter(grad_up_bias, "fsdp", scatter_dimension=0, tiled=True),
        lax.psum_scatter(grad_out_bias, "fsdp", scatter_dimension=0, tiled=True),
        lax.psum_scatter(grad_down_bias, "fsdp", scatter_dimension=0, tiled=True),
        lax.psum_scatter(norm_sums[0], "fsdp", scatter_dimension=0, tiled=True),
        lax.psum_scatter(norm_sums[1], "fsdp", scatter_dimension=0, tiled=True),
        lax.psum_scatter(norm_sums[2], "fsdp", scatter_dimension=0, tiled=True),
        lax.psum_scatter(norm_sums[3], "fsdp", scatter_dimension=0, tiled=True),
    )
    return (
        output,
        grad_tokens,
        shards[0],
        shards[1],
        shards[2],
        shards[3],
        shards[4],
        shards[5],
        shards[6],
        shards[7],
        shards[8],
        shards[9],
        shards[10],
        shards[11],
        shards[12],
        shards[13],
        shards[14],
    )


def solution(mesh):
    return jax.shard_map(
        local,
        mesh=mesh,
        in_specs=(
            P(("fsdp", "tensor"), None),
            P(("fsdp", "tensor"), None),
            P("fsdp", "tensor"),
            P("fsdp", "tensor"),
            P("fsdp", "tensor"),
            P("tensor", "fsdp"),
            P("fsdp", "tensor"),
            P("tensor", "fsdp"),
            P(("tensor", "fsdp")),
            P(("tensor", "fsdp")),
            P(("tensor", "fsdp")),
            P("fsdp"),
            P("fsdp"),
            P("fsdp"),
            P("fsdp"),
            P("fsdp"),
            P("fsdp"),
        ),
        out_specs=(
            P(("fsdp", "tensor"), None),
            P(("fsdp", "tensor"), None),
            P("fsdp", "tensor"),
            P("fsdp", "tensor"),
            P("fsdp", "tensor"),
            P("tensor", "fsdp"),
            P("fsdp", "tensor"),
            P("tensor", "fsdp"),
            P(("tensor", "fsdp")),
            P(("tensor", "fsdp")),
            P(("tensor", "fsdp")),
            P("fsdp"),
            P("fsdp"),
            P("fsdp"),
            P("fsdp"),
            P("fsdp"),
            P("fsdp"),
        ),
        check_vma=False,
    )
```

profile of v0, /device:TPU:0, one launch (start us, length us, event | category | flops | bytes accessed | tf_op | source)
XLA Modules:
  0.0 972.1 jit_solution(1498440569108670071)
XLA Ops:
  19.0 27.7 %all-reduce.20 = (bf16[768]{0:T(1024)(128)(2,1)S(1)}, bf16[768]{0:T(1024)(128)(2,1)S(1)}, bf16[192]{0:T(256)(128)(2,1)S(1)}, bf16[192]{0:T(256)(128)(2,1)S(1)}, ...) all-reduce(bf16[768]{0:T(1024)(128)(2,1)S(1)} %dynamic-update-slice, ...), channel_id=1, replica_groups=mesh['fsdp'=8,'tensor'=4] {'fsdp'}, use_global_device_ids=true, to_apply=%add.4 | all-reduce | flops 5760 | bytes 23040
  47.6 8.2 all_gather.69
  55.8 10.0 %all_gather.64 = bf16[768,192]{1,0:T(8,128)(2,1)S(1)} all-gather(bf16[96,192]{1,0:T(8,128)(2,1)} %param.23), channel_id=1, replica_groups=mesh['fsdp'=8,'tensor'=4] {'fsdp'}, dimensions={0}, use_global_device_ids=true | all-gather | bytes 331776 | tf_op jit(solution)/shard_map/all_gather | solution.py:53
  65.8 8.8 all_gather.66
  74.6 9.5 all_gather.67
  92.6 33.6 %while.29 = (s32[]{:T(128)}, bf16[4,512,3,64]{1,3,2,0:T(8,128)(2,1)S(1)}, f32[4,3,512,1]{2,1,3,0:T(4,128)}, f32[4,3,512,1]{2,1,3,0:T(4,128)}, bf16[4,512,3,64]{1...) while((s32[]{:T(128)}, ...), condition=%wide.region_3.4_spmd, body=%wide.region_0.3_spmd.sunk | while | flops 833713152 | bytes 39778408 | solution.py:122
  131.1 59.5 %reduce-scatter.19.cloned.1.call-done = bf16[512,768]{1,0:T(8,128)(2,1)} async-done(((bf16[2048,768]{1,0:T(8,128)(2,1)}), bf16[512,768]{1,0:T(8,128)(2,1)}) %reduce-scatter.19.cloned.1.call-update) | async-done | bytes 786448 | tf_op jit(solution)/shard_map/reduce_scatter | solution.py:124
  197.8 61.4 %all-gather.9.cloned.1.call-done = bf16[2048,768]{1,0:T(8,128)(2,1)} async-done(((bf16[512,768]{1,0:T(8,128)(2,1)}), bf16[2048,768]{1,0:T(8,128)(2,1)}) %all-gather.9.cloned.1.call-update) | async-done | bytes 3145744 | tf_op jit(solution)/shard_map/all_gather | solution.py:134
  259.2 19.0 %multiply_convert_fusion.1 = (bf16[2048,768]{1,0:T(8,128)(2,1)}, f32[2048,768]{1,0:T(8,128)}, f32[2048,768]{1,0:T(8,128)}) fusion(f32[768]{0:T(1024)} %convert_element_type.155, bf16[2048,768]{1,0:T(8,128)(2,1)} %all-gather.9.cloned.1.call-done, bf16[768,768]{1,0:T(8,128)(2,1)} %all-gather.11.cloned.1.call-done), kind=kOutput, calls=%fused_computation.51 | convolution fusion | flops 2519728128 | bytes 20057088 | tf_op jit(solution)/shard_map/dot_general | solution.py:135
  283.5 6.6 convolution_convert_fusion.1
  293.9 56.5 %reduce-scatter.21.cloned.1.call-done = bf16[512,768]{1,0:T(8,128)(2,1)} async-done(((bf16[2048,768]{1,0:T(8,128)(2,1)}), bf16[512,768]{1,0:T(8,128)(2,1)}) %reduce-scatter.21.cloned.1.call-update) | async-done | bytes 786448 | tf_op jit(solution)/shard_map/reduce_scatter | solution.py:140
  358.5 63.1 %all-gather.15.cloned.1.call-done = bf16[2048,768]{1,0:T(8,128)(2,1)} async-done(((bf16[512,768]{1,0:T(8,128)(2,1)}), bf16[2048,768]{1,0:T(8,128)(2,1)}) %all-gather.15.cloned.1.call-update) | async-done | bytes 3145744 | tf_op jit(solution)/shard_map/all_gather | solution.py:160
  421.6 11.1 %convert_reduce_fusion.2 = (f32[768]{0:T(1024)}, bf16[2048,768]{1,0:T(8,128)(2,1)S(1)}) fusion(f32[2048,768]{1,0:T(8,128)} %get-tuple-element.323, f32[2048,768]{1,0:T(8,128)} %get-tuple-element.335, f32[768]{0:T(1024)} %convert_element_type.155, bf16[2048,768]{1,0:T(8,128)(2,1)} %all-gather.15.cloned.1.call-done, ...), kind=kOutput, calls=%fused_computation.48 | convolution fusion | flops 2442657024 | bytes 20060160 | tf_op jit(solution)/shard_map/dot_general | solution.py:30
  438.5 59.0 %reduce-scatter.23.cloned.1.call-done = bf16[512,768]{1,0:T(8,128)(2,1)} async-done(((bf16[2048,768]{1,0:T(8,128)(2,1)}), bf16[512,768]{1,0:T(8,128)(2,1)}) %reduce-scatter.23.cloned.1.call-update) | async-done | bytes 786448 | tf_op jit(solution)/shard_map/reduce_scatter | solution.py:169
  505.6 63.5 %all-gather.17.cloned.1.call-done = bf16[2048,768]{1,0:T(8,128)(2,1)} async-done(((bf16[512,768]{1,0:T(8,128)(2,1)}), bf16[2048,768]{1,0:T(8,128)(2,1)}) %all-gather.17.cloned.1.call-update) | async-done | bytes 3145744 | tf_op jit(solution)/shard_map/all_gather | solution.py:176
  583.8 104.7 %while.30 = (s32[]{:T(128)}, f32[2048,3,64]{0,2,1:T(8,128)S(1)}, f32[2048,3,64]{0,2,1:T(8,128)}, bf16[4,512,3,64]{1,3,2,0:T(8,128)(2,1)}, bf16[4,512,3,64]{1,3,2...) while((s32[]{:T(128)}, f32[2048,3,64]{0,2,1:T(8,128)S(1)}, ...), condition=%wide.region_17.18_spmd.clone, body=%wide.region_15.17_spmd.clone.sunk | while | flops 2043738624 | bytes 119787768 | solution.py:208
  587.4 6.6 multiply_reduce_fusion.9
  599.7 6.2 fusion.138
  613.6 6.6 multiply_reduce_fusion.9
  625.9 6.1 fusion.138
  639.7 6.6 multiply_reduce_fusion.9
  651.9 6.1 fusion.138
  665.8 6.6 multiply_reduce_fusion.9
  696.2 7.0 fusion.61
  703.2 6.9 fusion.62
  723.7 18.4 %all-reduce.14 = bf16[16,768]{1,0:T(8,128)(2,1)S(1)} all-reduce(bf16[16,768]{1,0:T(8,128)(2,1)S(1)} %convert_element_type.180), channel_id=17, replica_groups=mesh['fsdp'=8,'tensor'=4] {'tensor'}, use_global_device_ids=true, to_apply=%region_39.40.clone | all-reduce | flops 12288 | bytes 49152
  749.0 22.4 %all-reduce.19 = (f32[192]{0:T(256)S(1)}, f32[192]{0:T(256)S(1)}, f32[768]{0:T(1024)S(1)}, f32[768]{0:T(1024)S(1)}, f32[768]{0:T(1024)S(1)}, /*index=5*/f32[768]...) all-reduce(f32[192]{0:T(256)S(1)} %reduce_sum.216, ...), channel_id=12, replica_groups=mesh['fsdp'=8,'tensor'=4] {'fsdp'}, use_global_device_ids=true, to_apply=%region_26.27.clone | all-reduce | flops 5760 | bytes 46080
  780.8 21.3 %reduce-scatter.27.cloned.1.call-done = f32[96,768]{1,0:T(8,128)} async-done(((f32[768,768]{1,0:T(8,128)}), f32[96,768]{1,0:T(8,128)}) %reduce-scatter.27.cloned.1.call-update) | async-done | bytes 294928 | tf_op jit(solution)/shard_map/reduce_scatter | solution.py:242
  802.2 46.5 %reduce-scatter.29.cloned.1.call-done = f32[768,96]{0,1:T(8,128)} async-done(((f32[768,768]{0,1:T(8,128)}), f32[768,96]{0,1:T(8,128)}) %reduce-scatter.29.cloned.1.call-update) | async-done | bytes 294928 | tf_op jit(solution)/shard_map/reduce_scatter | solution.py:243
  848.7 38.7 %reduce-scatter.31.cloned.1.call-done = f32[96,192]{1,0:T(8,128)} async-done(((f32[768,192]{1,0:T(8,128)}), f32[96,192]{1,0:T(8,128)}) %reduce-scatter.31.cloned.1.call-update) | async-done | bytes 73744
  887.4 38.6 %reduce-scatter.33.cloned.1.call-done = f32[96,192]{1,0:T(8,128)} async-done(((f32[768,192]{1,0:T(8,128)}), f32[96,192]{1,0:T(8,128)}) %reduce-scatter.33.cloned.1.call-update) | async-done | bytes 73744
  926.0 38.7 %reduce-scatter.35.cloned.1.call-done = f32[96,192]{1,0:T(8,128)} async-done(((f32[768,192]{1,0:T(8,128)}), f32[96,192]{1,0:T(8,128)}) %reduce-scatter.35.cloned.1.call-update) | async-done | bytes 73744
  (273 shorter events, 204.8 us)
Async XLA Ops:
  8.0 76.1 %all-gather.7.cloned.1.call-start = ((), (), s32[]{:S(2)}) async-start(), calls=%async_computation.10 | async-start | bytes 3932160 | tf_op jit(solution)/shard_map/all_gather | solution.py:92
  8.8 181.8 %reduce-scatter.19.cloned.1.call-start = ((), (), s32[]{:S(2)}) async-start(), calls=%async_computation.11 | async-start | bytes 3932160 | tf_op jit(solution)/shard_map/reduce_scatter | solution.py:124
  65.8 18.3 %copy-start.19 = (bf16[768,192]{1,0:T(8,128)(2,1)}, bf16[768,192]{1,0:T(8,128)(2,1)S(1)}, u32[]{:S(2)}) copy-start(bf16[768,192]{1,0:T(8,128)(2,1)S(1)} %all_gather.64) | copy-start | bytes 884740
  74.6 13.5 %copy-start.15 = (bf16[768,192]{1,0:T(8,128)(2,1)}, bf16[768,192]{1,0:T(8,128)(2,1)S(1)}, u32[]{:S(2)}) copy-start(bf16[768,192]{1,0:T(8,128)(2,1)S(1)} %all_gather.66) | copy-start | bytes 884740
  84.1 7.2 copy-start.21
  127.1 63.5 %copy-start.4 = (bf16[512,768]{1,0:T(8,128)(2,1)S(1)}, bf16[512,768]{1,0:T(8,128)(2,1)}, u32[]{:S(2)}) copy-start(bf16[512,768]{1,0:T(8,128)(2,1)} %param.21) | copy-start | bytes 2359300
  129.9 67.9 %all-gather.11.cloned.1.call-start = ((), (), s32[]{:S(2)}) async-start(), calls=%async_computation.13 | async-start | bytes 1327104 | tf_op jit(solution)/shard_map/all_gather | solution.py:57
  130.5 128.7 %all-gather.9.cloned.1.call-start = ((), (), s32[]{:S(2)}) async-start(), calls=%async_computation.12 | async-start | bytes 3932160 | tf_op jit(solution)/shard_map/all_gather | solution.py:134
  195.7 87.8 %all-gather.13.cloned.1.call-start = ((), (), s32[]{:S(2)}) async-start(), calls=%async_computation.14 | async-start | bytes 1327104 | tf_op jit(solution)/shard_map/all_gather | solution.py:58
  196.3 154.2 %reduce-scatter.21.cloned.1.call-start = ((), (), s32[]{:S(2)}) async-start(), calls=%async_computation.15 | async-start | bytes 3932160 | tf_op jit(solution)/shard_map/reduce_scatter | solution.py:140
  290.1 131.6 %all-gather.15.cloned.1.call-start = ((), (), s32[]{:S(2)}) async-start(), calls=%async_computation.16 | async-start | bytes 3932160 | tf_op jit(solution)/shard_map/all_gather | solution.py:160
  358.1 139.5 %reduce-scatter.23.cloned.1.call-start = ((), (), s32[]{:S(2)}) async-start(), calls=%async_computation.17 | async-start | bytes 3932160 | tf_op jit(solution)/shard_map/reduce_scatter | solution.py:169
  421.6 12.8 %copy-start.34 = (bf16[768,768]{1,0:T(8,128)(2,1)S(1)}, bf16[768,768]{1,0:T(8,128)(2,1)}, u32[]{:S(2)}) copy-start(bf16[768,768]{1,0:T(8,128)(2,1)} %all-gather.11.cloned.1.call-done) | copy-start | bytes 3538948
  438.5 130.6 %all-gather.17.cloned.1.call-start = ((), (), s32[]{:S(2)}) async-start(), calls=%async_computation.18 | async-start | bytes 3932160 | tf_op jit(solution)/shard_map/all_gather | solution.py:176
  505.5 271.2 %reduce-scatter.37.cloned.1.call-start = ((), (), s32[]{:S(2)}) async-start(), calls=%async_computation.25 | async-start | bytes 884736
  573.5 204.9 %reduce-scatter.25.cloned.1.call-start = ((), (), s32[]{:S(2)}) async-start(), calls=%async_computation.19 | async-start | bytes 3932160 | tf_op jit(solution)/shard_map/reduce_scatter | solution.py:229
  594.0 5.6 copy-start
  620.2 5.6 copy-start
  646.3 5.6 copy-start
  672.4 5.6 copy-start
  696.1 106.0 %reduce-scatter.27.cloned.1.call-start = ((), (), s32[]{:S(2)}) async-start(), calls=%async_computation.20 | async-start | bytes 2654208 | tf_op jit(solution)/shard_map/reduce_scatter | solution.py:242
  703.1 145.6 %reduce-scatter.29.cloned.1.call-start = ((), (), s32[]{:S(2)}) async-start(), calls=%async_computation.21 | async-start | bytes 2654208 | tf_op jit(solution)/shard_map/reduce_scatter | solution.py:243
  710.1 177.3 %reduce-scatter.31.cloned.1.call-start = ((), (), s32[]{:S(2)}) async-start(), calls=%async_computation.22 | async-start | bytes 884736
  714.1 4.3 copy-start.35
  714.1 6.2 copy-start.14
  714.1 7.0 copy-start.30
  714.1 211.9 %reduce-scatter.33.cloned.1.call-start = ((), (), s32[]{:S(2)}) async-start(), calls=%async_computation.23 | async-start | bytes 884736
  716.9 6.7 copy-start.32
  716.9 6.7 copy-start.31
  718.1 246.6 %reduce-scatter.35.cloned.1.call-start = ((), (), s32[]{:S(2)}) async-start(), calls=%async_computation.24 | async-start | bytes 884736
  744.9 33.4 %copy-start.9 = (f32[512,768]{1,0:T(8,128)S(1)}, f32[512,768]{1,0:T(8,128)}, u32[]{:S(2)}) copy-start(f32[512,768]{1,0:T(8,128)} %copy-done.8) | copy-start | bytes 4718596
  744.9 33.4 %copy-start.27 = (f32[512]{0:T(512)S(1)}, f32[512]{0:T(512)}, u32[]{:S(2)}) copy-start(f32[512]{0:T(512)} %copy-done.26) | copy-start | bytes 6148
  (30 other events, 74.2 us)
Sparse Core Ops, SparseCore 0:
  10.4 66.1 all-gather.6
  130.0 60.5 reduce-scatter.18
  358.2 63.4 all-gather.14
  505.6 63.4 all-gather.16
Sparse Core Ops, SparseCore 1:
  132.2 24.1 all-gather.10
  195.8 63.3 all-gather.8
  260.9 22.5 all-gather.12
  290.2 60.2 reduce-scatter.20
  438.6 58.9 reduce-scatter.22
  573.6 33.6 reduce-scatter.36
  696.2 59.8 reduce-scatter.24
  759.9 42.2 reduce-scatter.26
  806.3 42.3 reduce-scatter.28
  852.4 34.9 reduce-scatter.30
  891.0 34.9 reduce-scatter.32
  929.7 34.9 reduce-scatter.34
where the time goes:
time: 977 us; the launch traced here: 972 us
  waiting for transfers between devices  554 us (57%)
  matrix products  186 us (19%)
  blocking collectives  105 us (11%)
  other arithmetic  63.6 us (7%)
  local copies, waits for them, and re-layouts  41.2 us (4%)
  between operations  19.5 us (2%)
    unnamed x20, waiting for transfers between devices  118 us
    unnamed x3, blocking collectives  68.6 us
    all_gather x1, waiting for transfers between devices, local(): lax.all_gather(grad_resid_attn.astype(jnp.bfloat16), 'tensor', axis=0, ti...  63.5 us
    all_gather x1, waiting for transfers between devices, local(): lax.all_gather(grad_resid_ffn.astype(jnp.bfloat16), 'tensor', axis=0, til...  63.1 us
    all_gather x1, waiting for transfers between devices, local(): lax.all_gather(hidden.astype(jnp.bfloat16), 'tensor', axis=0, tiled=True)  61.4 us
    reduce_scatter x1, waiting for transfers between devices, local(): lax.psum_scatter(jnp.dot(attended, out_weight, preferred_element_type=jnp...  59.5 us
    reduce_scatter x1, waiting for transfers between devices, local(): lax.psum_scatter(times_transposed(grad_pre, back_up).astype(jnp.bfloat16)...  59 us
    reduce_scatter x1, waiting for transfers between devices, local(): lax.psum_scatter(jnp.dot(activ_low, down_weight, preferred_element_type=j...  56.5 us
  transfers between devices with their start and end apart: 16, of which 12 were waited for; matrix products, arithmetic and copies ran while one was open for 21% of the time, Pallas kernels for 0%

commit v1 on v0

--- a/solution.py
+++ b/solution.py
@@ -1,14 +1,680 @@
+import functools
+
 import jax
 import jax.numpy as jnp
+import numpy as np
 from jax import lax
+from jax.experimental import pallas as pl
+from jax.experimental.pallas import tpu as pltpu
 from jax.sharding import PartitionSpec as P
 
+F32, BF16 = jnp.float32, jnp.bfloat16
 HEAD = 64
-
-
 EPSILON = 1e-12
-CONTRACT_LAST = (((1,), (1,)), ((), ()))
-CONTRACT_FIRST = (((0,), (0,)), ((), ()))
+VMEM_LIMIT = 64000 * 1024
+
+
+def dot(left, right, contract):
+    return lax.dot_general(left, right, ((contract[:1], contract[1:]), ((), ())), preferred_element_type=F32)
+
+NN, NT, TN = (1, 0), (1, 1), (0, 0)
+
+
+def lanes_from(shape, low):
+    return lax.broadcasted_iota(jnp.int32, shape, len(shape) - 1) % (2 * HEAD) >= HEAD if not low else \
+        lax.broadcasted_iota(jnp.int32, shape, len(shape) - 1) % (2 * HEAD) < HEAD
+
+
+def project_keys(x, w, bias):
+    return (dot(x, w, NN) + bias).astype(BF16)
+
+
+def project_query(x, w, bias):
+    out = dot(x, w, NN) + bias
+    return jnp.where(lanes_from(out.shape, True), out.astype(BF16) * BF16(HEAD ** -0.5), BF16(0))
+
+
+def attend_kernel(heads, x_all, x_own, w_kv, w_qo, b_kv, b_q, kv_out, q_out, att_out, inv_out, exp_out, s_ref):
+    kv_out[0] = project_keys(x_all[...], w_kv[0], b_kv[0])
+    q_out[0] = project_query(x_own[...], w_qo[0], b_q[0])
+    for h in range(heads):
+        cols = slice(h * 128, h * 128 + 128)
+        kv = kv_out[0, :, cols]
+        s_ref[...] = dot(kv, q_out[0, :, cols], NT)
+        top = jnp.max(s_ref[...], axis=0, keepdims=True)
+        exps = jnp.exp(s_ref[...] - top)
+        inv = 1.0 / jnp.sum(exps, axis=0, keepdims=True)
+        exp_out[0, h] = exps.astype(BF16)
+        out = dot(kv, exp_out[0, h], TN) * inv
+        out = jnp.where(lax.broadcasted_iota(jnp.int32, out.shape, 0) >= HEAD, out, 0.0)
+        att_out[0, :, cols] = out.T.astype(BF16)
+        inv_out[0, h:h + 1] = inv
+
+
+def attend(x_all, x_own, w_kv, w_qo, b_kv, b_q):
+    groups, model, width = w_kv.shape
+    heads = width // 128
+    keys, rows = x_all.shape[0], x_own.shape[0]
+    whole = lambda n: pl.BlockSpec((n, model), lambda g: (0, 0))
+    lead = lambda *s: pl.BlockSpec((1, *s), lambda g: (g, *[0] * len(s)))
+    return pl.pallas_call(
+        functools.partial(attend_kernel, heads),
+        grid=(groups,),
+        in_specs=[whole(keys), whole(rows), lead(model, width), lead(model, width), lead(1, width), lead(1, width)],
+        out_specs=[lead(keys, width), lead(rows, width), lead(rows, width), lead(8, rows), lead(heads, keys, rows)],
+        out_shape=[jax.ShapeDtypeStruct(s, d) for s, d in [
+            ((groups, keys, width), BF16), ((groups, rows, width), BF16), ((groups, rows, width), BF16),
+            ((groups, 8, rows), F32), ((groups, heads, keys, rows), BF16)]],
+        scratch_shapes=[pltpu.VMEM((keys, rows), F32)],
+        compiler_params=pltpu.CompilerParams(vmem_limit_bytes=VMEM_LIMIT),
+    )(x_all, x_own, w_kv, w_qo, b_kv, b_q)
+
+
+def norm_forward(z):
+    mean = jnp.mean(z, -1, keepdims=True)
+    centered = z - mean
+    inv = lax.rsqrt(jnp.mean(centered * centered, -1, keepdims=True) + EPSILON)
+    return centered * inv, inv
+
+
+def norm_backward(n, inv, dn):
+    return inv * (dn - jnp.mean(dn, -1, keepdims=True) - n * jnp.mean(dn * n, -1, keepdims=True))
+
+
+def colsum(x):
+    return jnp.sum(x.astype(F32), axis=0, keepdims=True)
+
+
+def ffn_kernel(groups, x_own, cot, att, w_qo, w_up0, w_up1, w_dn0, w_dn1, b_up, vecs,
+               out_ref, resid_ref, datt_ref, g_o, g_up0, g_up1, g_dn0, g_dn1, g_bup, g_vecs,
+               act_ref, slope_ref, hid_ref, n1_ref, acc_ref, low_ref, hl_ref):
+    ups, downs, g_ups, g_dns = (w_up0, w_up1), (w_dn0, w_dn1), (g_up0, g_up1), (g_dn0, g_dn1)
+    vec = lambda k: vecs[k:k + 1, :]
+    width = w_up0.shape[2]
+    acc_ref[...] = x_own[...].astype(F32) + vec(0)
+    def branch(g, c):
+        acc_ref[...] += dot(att[g], w_qo[g], NT)
+        return c
+    lax.fori_loop(0, groups, branch, 0)
+    n1, inv1 = norm_forward(acc_ref[...])
+    n1_ref[...] = n1
+    hidden = n1 * vec(2) + vec(3)
+    hid_ref[...] = hidden
+    hl_ref[...] = hidden.astype(BF16)
+    acc_ref[...] = hidden + vec(1)
+    def forward(g, c):
+        for k in range(2):
+            pre = dot(hl_ref[...], ups[k][g], NN) + b_up[g, :, k * width:(k + 1) * width]
+            phi = 0.5 + 0.5 * lax.erf(pre * np.float32(0.5 ** 0.5))
+            slope_ref[g, k] = phi + pre * (jnp.exp(-0.5 * pre * pre) * np.float32((2 * np.pi) ** -0.5))
+            act_ref[g, k] = (pre * phi).astype(BF16)
+            acc_ref[...] += dot(act_ref[g, k], downs[k][g], NT)
+        return c
+    lax.fori_loop(0, groups, forward, 0)
+    n2, inv2 = norm_forward(acc_ref[...])
+    out_ref[...] = n2 * vec(4) + vec(5)
+    cott = cot[...].astype(F32)
+    g_vecs[4:5] = colsum(cott * n2)
+    g_vecs[5:6] = colsum(cott)
+    resid = norm_backward(n2, inv2, cott * vec(4))
+    acc_ref[...] = resid
+    low_ref[...] = resid.astype(BF16)
+    g_vecs[1:2] = colsum(low_ref[...])
+    def backward(g, c):
+        for k in range(2):
+            g_dns[k][g] = dot(low_ref[...], act_ref[g, k], TN).astype(BF16)
+            gp = (dot(low_ref[...], downs[k][g], NN) * slope_ref[g, k]).astype(BF16)
+            act_ref[g, k] = gp
+            g_bup[g, :, k * width:(k + 1) * width] = colsum(gp)
+            g_ups[k][g] = dot(hl_ref[...], gp, TN).astype(BF16)
+            acc_ref[...] += dot(act_ref[g, k], ups[k][g], NT)
+        return c
+    lax.fori_loop(0, groups, backward, 0)
+    gh = acc_ref[...]
+    g_vecs[2:3] = colsum(gh * n1_ref[...])
+    g_vecs[3:4] = colsum(gh)
+    ga = norm_backward(n1_ref[...], inv1, gh * vec(2))
+    resid_ref[...] = ga
+    low_ref[...] = ga.astype(BF16)
+    g_vecs[0:1] = colsum(low_ref[...])
+    def last(g, c):
+        da = dot(low_ref[...], w_qo[g], NN)
+        datt_ref[g] = jnp.where(lanes_from(da.shape, False), da, 0.0).astype(BF16)
+        g_o[g] = dot(low_ref[...], att[g], TN).astype(BF16)
+        return c
+    lax.fori_loop(0, groups, last, 0)
+
+
+def feed_forward(x_own, cot, att, w_qo, ups, downs, b_up, vecs):
+    groups, model, width = w_qo.shape
+    rows = x_own.shape[0]
+    vm = pl.BlockSpec(memory_space=pltpu.VMEM)
+    wshape = ((groups, model, width), BF16)
+    return pl.pallas_call(
+        functools.partial(ffn_kernel, groups),
+        in_specs=[vm] * 10, out_specs=[vm] * 10,
+        out_shape=[jax.ShapeDtypeStruct(s, d) for s, d in [
+            ((rows, model), F32), ((rows, model), F32), ((groups, rows, width), BF16),
+            wshape, wshape, wshape, wshape, wshape, ((groups, 1, 2 * width), F32), ((8, model), F32)]],
+        scratch_shapes=[pltpu.VMEM((groups, 2, rows, width), BF16), pltpu.VMEM((groups, 2, rows, width), F32),
+                        pltpu.VMEM((rows, model), F32), pltpu.VMEM((rows, model), F32), pltpu.VMEM((rows, model), F32),
+                        pltpu.VMEM((rows, model), BF16), pltpu.VMEM((rows, model), BF16)],
+        compiler_params=pltpu.CompilerParams(vmem_limit_bytes=VMEM_LIMIT),
+    )(x_own, cot, att, w_qo, *ups, *downs, b_up, vecs)
+
+
+def backward_kernel(groups, heads, blocks, x_all, x_own, w_kv, w_qo, kv, q, att, inv, datt, g_o, e_ref,
+                    dx_ref, dxo_ref, g_kv, g_qo, g_bkv, g_bq,
+                    do_ref, r_ref, dqt_ref, dkv_ref, acc_ref, wacc_ref):
+    b, g = pl.program_id(0), pl.program_id(1)
+    rows = x_own.shape[0]
+    @pl.when(b == 0)
+    def _():
+        for h in range(heads):
+            cols = slice(h * 128, h * 128 + 128)
+            da = datt[g, :, cols].astype(F32).T
+            scale = inv[g, h:h + 1]
+            prod = jnp.sum(da * att[g, :, cols].astype(F32).T, axis=0, keepdims=True)
+            r_ref[g, h:h + 1] = prod * scale
+            do_ref[g, :, cols] = (da * scale).T.astype(BF16)
+            dqt_ref[g, h] = jnp.zeros_like(dqt_ref[g, h])
+        wacc_ref[g] = jnp.zeros_like(wacc_ref[g])
+        g_bkv[g] = jnp.zeros_like(g_bkv[g])
+    @pl.when(g == 0)
+    def _():
+        acc_ref[...] = jnp.zeros_like(acc_ref)
+    here = pl.ds(pl.multiple_of(b * rows, rows), rows)
+    for h in range(heads):
+        cols = slice(h * 128, h * 128 + 128)
+        k = kv[g, here, cols]
+        d = do_ref[g, :, cols]
+        e = e_ref[0, h]
+        ds = (e.astype(F32) * (dot(k, d, NT) - r_ref[g, h:h + 1])).astype(BF16)
+        dkv_ref[:, cols] = (dot(ds, q[g, :, cols], NN) + dot(e, d, NN)).astype(BF16)
+        dqt_ref[g, h] += dot(k, ds, TN)
+    dk = dkv_ref[...]
+    g_bkv[g] += colsum(dk)
+    acc_ref[...] += dot(dk, w_kv[g], NT)
+    wacc_ref[g] += dot(x_all[here, :], dk, TN)
+    @pl.when(g == groups - 1)
+    def _():
+        dx_ref[0] = acc_ref[...].astype(BF16)
+    @pl.when(b == blocks - 1)
+    def _():
+        g_kv[g] = wacc_ref[g].astype(BF16)
+        for h in range(heads):
+            cols = slice(h * 128, h * 128 + 128)
+            dq = dqt_ref[g, h] * np.float32(HEAD ** -0.5)
+            dq = jnp.where(lax.broadcasted_iota(jnp.int32, dq.shape, 0) < HEAD, dq, 0.0)
+            dkv_ref[:, cols] = dq.T.astype(BF16)
+        dq = dkv_ref[...]
+        g_bq[g] = colsum(dq)
+        @pl.when(g == 0)
+        def _():
+            dxo_ref[...] = jnp.zeros_like(dxo_ref)
+        dxo_ref[...] += dot(dq, w_qo[g], NT)
+        g_qo[g] = (dot(x_own[...], dq, TN) + g_o[g].astype(F32)).astype(BF16)
+
+
+def backward(x_all, x_own, w_kv, w_qo, kv, q, att, inv, datt, g_o, e):
+    groups, model, width = w_kv.shape
+    heads, rows = width // 128, x_own.shape[0]
+    blocks = x_all.shape[0] // rows
+    vm = pl.BlockSpec(memory_space=pltpu.VMEM)
+    wshape = ((groups, model, width), BF16)
+    return pl.pallas_call(
+        functools.partial(backward_kernel, groups, heads, blocks),
+        grid=(blocks, groups),
+        in_specs=[vm] * 10 + [pl.BlockSpec((1, heads, rows, rows), lambda b, g: (g, 0, b, 0))],
+        out_specs=[pl.BlockSpec((1, rows, model), lambda b, g: (b, 0, 0))] + [vm] * 5,
+        out_shape=[jax.ShapeDtypeStruct(s, d) for s, d in [
+            ((blocks, rows, model), BF16), ((rows, model), F32), wshape, wshape,
+            ((groups, 1, width), F32), ((groups, 1, width), F32)]],
+        scratch_shapes=[pltpu.VMEM((groups, rows, width), BF16), pltpu.VMEM((groups, 8, rows), F32),
+                        pltpu.VMEM((groups, heads, 128, rows), F32), pltpu.VMEM((rows, width), BF16),
+                        pltpu.VMEM((rows, model), F32), pltpu.VMEM((groups, model, width), F32)],
+        compiler_params=pltpu.CompilerParams(vmem_limit_bytes=VMEM_LIMIT),
+    )(x_all, x_own, w_kv, w_qo, kv, q, att, inv, datt, g_o, e)
+
+
+MESH = pl.DeviceIdType.MESH
+ANY = pl.BlockSpec(memory_space=pl.ANY)
+VM = pl.BlockSpec(memory_space=pltpu.VMEM)
+
+
+def flip(index, bit):
+    return index + bit - 2 * bit * lax.rem(index // bit, 2)
+
+
+def flips(index, mask):
+    bit = 1
+    while bit <= mask:
+        if mask & bit:
+            index = flip(index, bit)
+        bit *= 2
+    return index
+
+
+def span(bits):
+    masks = [0]
+    for bit in bits:
+        masks += [m | bit for m in masks]
+    return masks
+
+
+def orders(fsdp):
+    bits = [1 << k for k in range(fsdp.bit_length() - 1)]
+    return bits[1:] + bits[:1], bits[:0:-1] + bits[:1]
+
+
+class Place:
+    def __init__(self, fsdp, tensor):
+        self.fsdp, self.tensor = fsdp, tensor
+        self.i, self.j = lax.axis_index("fsdp"), lax.axis_index("tensor")
+        self.half = tensor // 2
+        self.c = lax.rem(self.i, 2)
+        self.h = self.j // self.half
+        self.on = self.c == self.h
+        self.off = self.c != self.h
+        self.twin = flip(self.i, 1)
+        self.swap = lax.rem(self.j + self.half, tensor)
+        self.block = jnp.where(self.on, self.j, self.swap)
+        self.edge = self.half - 1 + self.c
+        self.end = self.c * (tensor - 1)
+        self.mate = self.h * tensor + 1 - self.j
+        self.is_edge = self.j == self.edge
+        self.is_end = self.j == self.end
+
+    def other(self, k):
+        return (1 - self.c) * (self.half + k) + self.c * (self.half - 1 - k)
+
+    def barrier(self):
+        sem = pltpu.get_barrier_semaphore()
+        others = [(self.i, lax.rem(self.j + k, self.tensor)) for k in range(1, self.tensor)]
+        bit = 1
+        while bit < self.fsdp:
+            others.append((flip(self.i, bit), self.j))
+            bit *= 2
+        others.append((self.twin, self.swap))
+        for i, j in others:
+            pl.semaphore_signal(sem, inc=1, device_id=(i, j), device_id_type=MESH)
+        pl.semaphore_wait(sem, len(others))
+
+
+class Sends:
+    def __init__(self, place, send, recv):
+        self.place, self.send, self.recv, self.n, self.started = place, send, recv, 0, []
+
+    def slot(self):
+        self.n += 1
+        return self.n - 1
+
+    def copy(self, src, dst, slot, i, j):
+        return pltpu.make_async_remote_copy(src_ref=src, dst_ref=dst, send_sem=self.send.at[slot], recv_sem=self.recv.at[slot],
+                                            device_id=(i, j), device_id_type=MESH)
+
+    def start(self, src, dst, slot, i, j, when=None):
+        copy = self.copy(src, dst, slot, i, j)
+        if when is None:
+            copy.start()
+        else:
+            pl.when(when)(copy.start)
+        self.started.append((copy, when))
+
+    def arrive(self, dst, slot, when=None):
+        copy = self.copy(dst, dst, slot, self.place.i, self.place.j)
+        if when is None:
+            copy.wait_recv()
+        else:
+            pl.when(when)(copy.wait_recv)
+
+    def finish(self):
+        for copy, when in self.started:
+            if when is None:
+                copy.wait_send()
+            else:
+                pl.when(when)(copy.wait_send)
+        self.started = []
+
+
+class Gather:
+    def __init__(self, sends, array, order, own=None):
+        self.s, self.p, self.a, self.order = sends, sends.place, array, order
+        self.own = own
+        self.right = [sends.slot() for _ in range(self.p.tensor - 1)]
+        self.left = [sends.slot() for _ in range(self.p.tensor - 1)]
+        self.stage = [[(m, sends.slot()) for m in span(order[:k])] for k in range(len(order))]
+
+    def line(self, step):
+        s, p, n = self.s, self.p, self.p.tensor
+        for slots, way in ((self.right, 1), (self.left, -1)):
+            owner = p.j - way * step
+            exists = (owner >= 0) & (owner < n)
+            there = p.j + way
+            block = self.a.at[owner, p.i]
+            if step > 0:
+                s.arrive(block, slots[step - 1], exists)
+            if step < n - 1:
+                src = self.own if step == 0 and self.own is not None else block
+                s.start(src, block, slots[step], p.i, there, exists & (there >= 0) & (there < n))
+
+    def slab(self, mask):
+        return self.a.at[:, flips(self.p.i, mask)]
+
+    def go(self, k, masks=None):
+        for m, slot in self.stage[k]:
+            if masks is None or m in masks:
+                self.s.start(self.slab(m), self.slab(m), slot, flip(self.p.i, self.order[k]), self.p.j)
+
+    def come(self, k):
+        for m, slot in self.stage[k]:
+            self.s.arrive(self.slab(m | self.order[k]), slot)
+
+
+def gather_kernel(fsdp, tensor, pack, small, tok, cot, w, sm, x, cotp, send, recv, local):
+    p = Place(fsdp, tensor)
+    s = Sends(p, send, recv)
+    first, second = orders(fsdp)
+    chunks = pack.shape[0]
+    gathers = [Gather(s, w.at[k], (first, second)[k % 2], pack.at[k]) for k in range(chunks)]
+    tiny = Gather(s, sm, first, small)
+    xin = [s.slot() for _ in range(tensor)]
+    xtwin = s.slot()
+    cslot = s.slot()
+    copies = [pltpu.make_async_copy(pack.at[k], w.at[k, p.j, p.i], local.at[k]) for k in range(chunks)]
+    copies += [pltpu.make_async_copy(small, sm.at[p.j, p.i], local.at[chunks]),
+               pltpu.make_async_copy(tok, x.at[p.j], local.at[chunks + 1])]
+    for copy in copies[:-1]:
+        copy.start()
+    pl.when(p.on)(copies[-1].start)
+    p.barrier()
+    g0, g1, g2 = [tiny] + gathers[:2], gathers[2:4], gathers[4:]
+    each = lambda group, call: [call(g) for g in group]
+    xslot = lambda t: s_slot(xin, t)
+
+    def x_start(src, t, i, j, when):
+        copy = pltpu.make_async_remote_copy(src_ref=src, dst_ref=x.at[t], send_sem=xsend(t, i), recv_sem=recv.at[xin[0] + t],
+                                            device_id=(i, j), device_id_type=MESH)
+        pl.when(when)(copy.start)
+        s.started.append((copy, when))
+
+    def xsend(t, i):
+        return send.at[xin[0] + t] if i is p.i else twin_send(t)
+
+    def twin_send(t):
+        return local.at[chunks + 2 + t]
+
+    def x_arrive(t, when):
+        pl.when(when)(pltpu.make_async_remote_copy(src_ref=x.at[t], dst_ref=x.at[t], send_sem=send.at[xin[0] + t], recv_sem=recv.at[xin[0] + t],
+                                                   device_id=(p.i, p.j), device_id_type=MESH).wait_recv)
+
+    each(g0, lambda g: g.line(0))
+    x_start(tok, p.j, p.i, p.edge, p.off)
+    if p.half > 1:
+        x_start(tok, p.j, p.i, p.mate, p.on)
+    x_start(tok, p.j, p.twin, p.j, p.on)
+    for step in range(1, tensor):
+        each(g0, lambda g: g.line(step))
+    for copy in copies[:-1]:
+        copy.wait()
+    each(g0, lambda g: g.go(0))
+    each(g1, lambda g: g.line(0))
+    each(g0, lambda g: g.come(0))
+    each(g0, lambda g: g.go(1))
+    each(g0, lambda g: g.go(2, span(g.order[:1])))
+    if p.half > 1:
+        x_arrive(p.mate, p.on)
+        x_start(x.at[p.mate], p.mate, p.twin, p.j, p.on)
+    for k in range(p.half):
+        t = p.other(k)
+        x_arrive(t, p.on)
+        if p.half > 1:
+            x_start(x.at[t], t, p.i, p.end, p.on & p.is_edge)
+        x_start(x.at[t], t, p.twin, p.j, p.on)
+        if k == 0:
+            each(g1, lambda g: g.line(1))
+            each(g0, lambda g: g.come(1))
+            each(g0, lambda g: g.go(2, [m for m in span(g.order[:2]) if m not in span(g.order[:1])]))
+            each(g2, lambda g: g.line(0))
+    for step in range(2, tensor):
+        each(g1, lambda g: g.line(step))
+    each(g1, lambda g: g.go(0))
+    s.start(cot, cotp, cslot, p.twin, p.swap, p.off)
+    each(g2, lambda g: g.line(1))
+    each(g1, lambda g: g.come(0))
+    each(g1, lambda g: g.go(1))
+    each(g1, lambda g: g.go(2, span(g.order[:1])))
+    for step in range(2, tensor):
+        each(g2, lambda g: g.line(step))
+    each(g2, lambda g: g.go(0))
+    each(g1, lambda g: g.come(1))
+    each(g1, lambda g: g.go(2, [m for m in span(g.order[:2]) if m not in span(g.order[:1])]))
+    each(g2, lambda g: g.come(0))
+    each(g2, lambda g: g.go(1))
+    each(g2, lambda g: g.go(2, span(g.order[:1])))
+    each(g2, lambda g: g.come(1))
+    each(g2, lambda g: g.go(2, [m for m in span(g.order[:2]) if m not in span(g.order[:1])]))
+    for group in (g0, g1, g2):
+        each(group, lambda g: g.come(2))
+    for t in range(tensor):
+        x_arrive(t, p.off)
+    s.arrive(cotp, cslot, p.off)
+    pl.when(p.on)(copies[-1].wait)
+    s.finish()
+
+
+def gather_all(fsdp, tensor, pack, small, tok, cot):
+    chunks, shard, width = pack.shape
+    rows, model = tok.shape
+    slots = (chunks + 1) * (2 * (tensor - 1) + fsdp - 1) + tensor + 2
+    return pl.pallas_call(
+        functools.partial(gather_kernel, fsdp, tensor),
+        in_specs=[VM, VM, VM, ANY], out_specs=[ANY] * 4,
+        out_shape=[jax.ShapeDtypeStruct(s, d) for s, d in [
+            ((chunks, tensor, fsdp, shard, width), BF16), ((tensor, fsdp, *small.shape), F32),
+            ((tensor, rows, model), BF16), ((rows, model), BF16)]],
+        scratch_shapes=[pltpu.SemaphoreType.DMA((slots,)), pltpu.SemaphoreType.DMA((slots,)),
+                        pltpu.SemaphoreType.DMA((chunks + 2 + tensor,))],
+        compiler_params=pltpu.CompilerParams(collective_id=0, has_side_effects=True, vmem_limit_bytes=VMEM_LIMIT),
+    )(pack, small, tok, cot)
+
+
+class Scatter:
+    def __init__(self, sends, parts, halves, from_left, from_right, order, out):
+        self.s, self.p, self.a, self.order = sends, sends.place, parts, order[::-1]
+        self.halves, self.left_in, self.right_in, self.out = halves, from_left, from_right, out
+        n, self.n = len(order), self.p.tensor
+        self.masks = [span(self.order[k + 1:]) for k in range(n)]
+        self.slots = [[sends.slot() for _ in self.masks[k]] for k in range(n)]
+        self.right = [sends.slot() for _ in range(self.n)]
+        self.left = [sends.slot() for _ in range(self.n)]
+
+    def part(self, k, mask):
+        if k == 0:
+            return self.a.at[:, flips(self.p.i, mask)]
+        return self.halves[k - 1].at[self.masks[k - 1].index(mask)]
+
+    def go(self, k):
+        bit = self.order[k]
+        for n, m in enumerate(self.masks[k]):
+            self.s.start(self.part(k, m | bit), self.halves[k].at[n], self.slots[k][n], flip(self.p.i, bit), self.p.j)
+
+    def come(self, k):
+        for n, m in enumerate(self.masks[k]):
+            here, mine = self.halves[k].at[n], self.part(k, m)
+            self.s.arrive(here, self.slots[k][n])
+            for t in range(self.n):
+                here[t] = (here[t].astype(F32) + mine[t].astype(F32)).astype(BF16)
+
+    def line(self, step):
+        s, p, n = self.s, self.p, self.n
+        total = self.halves[-1].at[0]
+        for slots, way, inbox in ((self.right, 1, self.left_in), (self.left, -1, self.right_in)):
+            far = n - 1 - step
+            owner = p.j + way * far
+            before = p.j - way
+            exists = (owner >= 0) & (owner < n)
+            has = exists & (before >= 0) & (before < n)
+            if far < n - 1:
+                s.arrive(inbox.at[owner], slots[far + 1], has)
+            if far > 0:
+                def add(owner=owner, inbox=inbox):
+                    inbox[owner] = (inbox[owner].astype(F32) + total[owner].astype(F32)).astype(BF16)
+                def plain(owner=owner, inbox=inbox):
+                    inbox[owner] = total[owner]
+                if far < n - 1:
+                    pl.when(has)(add)
+                    pl.when(exists & jnp.logical_not(has))(plain)
+                else:
+                    pl.when(exists)(plain)
+                s.start(inbox.at[owner], inbox.at[owner], slots[far], p.i, p.j + way, exists)
+
+    def result(self):
+        p = self.p
+        self.out[...] = self.halves[-1][0, p.j].astype(F32)
+        for inbox, before in ((self.left_in, p.j > 0), (self.right_in, p.j < self.n - 1)):
+            @pl.when(before)
+            def _(inbox=inbox):
+                self.out[...] += inbox[p.j].astype(F32)
+
+
+def reduce_kernel(fsdp, tensor, chunks, *refs):
+    grads, (dx, own, own2, result, tiny), refs = refs[:chunks], refs[chunks:chunks + 5], refs[chunks + 5:]
+    g_out, dx_out, out_out, tiny_out = refs[:4]
+    refs = refs[4:]
+    bits = fsdp.bit_length() - 1
+    halves, refs = refs[:bits], refs[bits:]
+    inl, inr, twin_in, mate_in, fin_in, send_out, recv_out, send_own, tiny_in, send, recv = refs
+    p = Place(fsdp, tensor)
+    s = Sends(p, send, recv)
+    first, second = orders(fsdp)
+    sc = [Scatter(s, grads[k], [h.at[k] for h in halves], inl.at[k], inr.at[k], (first, second)[k % 2], g_out.at[k]) for k in range(chunks)]
+    each = lambda group, call: [call(g) for g in group]
+    g1, g2, g0 = sc[4:], sc[2:4], sc[:2]
+    twin = [s.slot() for _ in range(tensor)]
+    mate = [s.slot() for _ in range(tensor)]
+    fin, swp = s.slot(), s.slot()
+    tiny_out[...] = tiny[...]
+    send_out[...] = result[...].astype(BF16)
+    @pl.when(p.off)
+    def _():
+        send_own[...] = (dx[p.block].astype(F32) + (own[...] + own2[...])).astype(BF16)
+    p.barrier()
+    for t in range(tensor):
+        s.start(dx.at[t], twin_in.at[t], twin[t], p.twin, p.j, p.off & (p.block != t))
+        s.start(send_own, twin_in.at[t], twin[t], p.twin, p.j, p.off & (p.block == t))
+    for g in (g1, g2, g0):
+        each(g, lambda g: g.go(0))
+    s.start(send_out, recv_out, swp, p.twin, p.swap, p.off)
+    for t in range(tensor):
+        @pl.when(p.on)
+        def _(t=t):
+            s.copy(twin_in.at[t], twin_in.at[t], twin[t], p.i, p.j).wait_recv()
+            twin_in[t] = (twin_in[t].astype(F32) + dx[t].astype(F32)).astype(BF16)
+    far = list(range(tensor // 2))[::-1]
+    if p.half > 1:
+        for k in far:
+            t = p.other(k)
+            s_copy = pltpu.make_async_remote_copy(src_ref=twin_in.at[t], dst_ref=mate_in.at[t], send_sem=send.at[mate[0] + t],
+                                                  recv_sem=recv.at[mate[0] + t], device_id=(p.i, p.edge), device_id_type=MESH)
+            when = p.on & p.is_end
+            pl.when(when)(s_copy.start)
+            s.started.append((s_copy, when))
+        s_copy = pltpu.make_async_remote_copy(src_ref=twin_in.at[p.mate], dst_ref=mate_in.at[p.mate], send_sem=send.at[mate[0] + p.mate],
+                                              recv_sem=recv.at[mate[0] + p.mate], device_id=(p.i, p.mate), device_id_type=MESH)
+        pl.when(p.on)(s_copy.start)
+        s.started.append((s_copy, p.on))
+    def x_wait(t, when):
+        pl.when(when)(pltpu.make_async_remote_copy(src_ref=mate_in.at[t], dst_ref=mate_in.at[t], send_sem=send.at[mate[0] + t],
+                                                   recv_sem=recv.at[mate[0] + t], device_id=(p.i, p.j), device_id_type=MESH).wait_recv)
+    each(g1, lambda g: g.come(0))
+    each(g1, lambda g: g.go(1))
+    for k in far:
+        t = p.other(k)
+        if p.half > 1:
+            x_wait(t, p.on & p.is_edge)
+            @pl.when(p.on & p.is_edge)
+            def _(t=t):
+                mate_in[t] = (mate_in[t].astype(F32) + twin_in[t].astype(F32)).astype(BF16)
+        src = mate_in if p.half > 1 else twin_in
+        copy = pltpu.make_async_remote_copy(src_ref=src.at[t], dst_ref=fin_in, send_sem=send.at[twin[0] + k], recv_sem=recv.at[fin],
+                                            device_id=(p.i, t), device_id_type=MESH)
+        when = p.on & p.is_edge
+        pl.when(when)(copy.start)
+        s.started.append((copy, when))
+    each(g2, lambda g: g.come(0))
+    each(g2, lambda g: g.go(1))
+    each(g1, lambda g: g.come(1))
+    each(g1, lambda g: g.go(2))
+    each(g0, lambda g: g.come(0))
+    each(g0, lambda g: g.go(1))
+    each(g2, lambda g: g.come(1))
+    each(g2, lambda g: g.go(2))
+    each(g1, lambda g: g.come(2))
+    each(g1, lambda g: g.line(0))
+    each(g0, lambda g: g.come(1))
+    each(g0, lambda g: g.go(2))
+    each(g1, lambda g: g.line(1))
+    each(g2, lambda g: g.come(2))
+    each(g2, lambda g: g.line(0))
+    for step in range(2, tensor):
+        each(g1, lambda g: g.line(step))
+    each(g1, lambda g: g.result())
+    each(g0, lambda g: g.come(2))
+    each(g0, lambda g: g.line(0))
+    for step in range(1, tensor):
+        each(g2, lambda g: g.line(step))
+    each(g2, lambda g: g.result())
+    for step in range(1, tensor):
+        each(g0, lambda g: g.line(step))
+    each(g0, lambda g: g.result())
+    bit, n = 1, 0
+    while bit < fsdp * tensor:
+        i, j = (flip(p.i, bit), p.j) if bit < fsdp else (p.i, flip(p.j, bit // fsdp))
+        slot = s.slot()
+        s.start(tiny_out, tiny_in.at[n], slot, i, j)
+        s.arrive(tiny_in.at[n], slot)
+        s.started.pop()[0].wait_send()
+        tiny_out[...] += tiny_in[n]
+        bit, n = bit * 2, n + 1
+    @pl.when(p.on)
+    def _():
+        dx_out[...] = own[...] + own2[...] + twin_in[p.j].astype(F32)
+        out_out[...] = result[...]
+    if p.half > 1:
+        x_wait(p.j, p.on)
+        @pl.when(p.on)
+        def _():
+            dx_out[...] += mate_in[p.j].astype(F32)
+    s.arrive(fin_in, fin, p.off)
+    s.arrive(recv_out, swp, p.off)
+    @pl.when(p.off)
+    def _():
+        dx_out[...] = fin_in[...].astype(F32)
+        out_out[...] = recv_out[...].astype(F32)
+    s.finish()
+
+
+def reduce_all(fsdp, tensor, grads, dx, own, own2, result, tiny):
+    chunks = len(grads)
+    shape = grads[0].shape
+    shard, width = shape[2:]
+    rows, model = own.shape
+    bits = fsdp.bit_length() - 1
+    slots = chunks * (fsdp - 1 + 2 * tensor) + 2 * tensor + 2 + 16
+    steps = (fsdp * tensor).bit_length() - 1
+    scratch = [pltpu.VMEM((chunks, fsdp >> (k + 1), tensor, shard, width), BF16) for k in range(bits)]
+    scratch += [pltpu.VMEM((chunks, tensor, shard, width), BF16)] * 2
+    scratch += [pltpu.VMEM((tensor, rows, model), BF16)] * 2 + [pltpu.VMEM((rows, model), BF16)] * 4
+    scratch += [pltpu.VMEM((steps, *tiny.shape), F32), pltpu.SemaphoreType.DMA((slots,)), pltpu.SemaphoreType.DMA((slots,))]
+    return pl.pallas_call(
+        functools.partial(reduce_kernel, fsdp, tensor, chunks),
+        in_specs=[VM] * (chunks + 5), out_specs=[VM] * 4,
+        out_shape=[jax.ShapeDtypeStruct(s, d) for s, d in [
+            ((chunks, shard, width), F32), ((rows, model), F32), ((rows, model), F32), (tiny.shape, F32)]],
+        scratch_shapes=scratch,
+        compiler_params=pltpu.CompilerParams(collective_id=1, has_side_effects=True, vmem_limit_bytes=VMEM_LIMIT),
+    )(*grads, dx, own, own2, result, tiny)
 
 
 def normalize(values, gain, shift):
@@ -23,14 +689,14 @@
 
 
 def outer_sum(left, right):
-    return lax.dot_general(left, right, CONTRACT_FIRST, preferred_element_type=jnp.float32)
+    return dot(left, right, TN)
 
 
 def times_transposed(left, right):
-    return lax.dot_general(left, right, CONTRACT_LAST, preferred_element_type=jnp.float32)
-
-
-def local(
+    return dot(left, right, NT)
+
+
+def plain(
     tokens,
     cotangent,
     w_query,
@@ -272,9 +938,84 @@
     )
 
 
+def fits(tokens, w_query, w_up):
+    fsdp, tensor = lax.axis_size("fsdp"), lax.axis_size("tensor")
+    shard, columns = w_query.shape
+    return (tensor in (2, 4) and fsdp >= 4 and fsdp & (fsdp - 1) == 0 and shard % 16 == 0 and columns % HEAD == 0
+            and w_up.shape[1] == 4 * columns and tokens.shape[0] % 128 == 0)
+
+
+def pairs(first, second):
+    rows, columns = first.shape
+    both = jnp.stack([first.reshape(rows, -1, HEAD), second.reshape(rows, -1, HEAD)], 2)
+    return both.reshape(rows, 2 * columns)
+
+
+def layer(tokens, cotangent, w_query, w_key, w_value, w_out, w_up, w_down, b_query, b_value, b_up, b_out, b_down,
+          gain_attn, shift_attn, gain_ffn, shift_ffn):
+    if not fits(tokens, w_query, w_up):
+        return plain(tokens, cotangent, w_query, w_key, w_value, w_out, w_up, w_down, b_query, b_value, b_up, b_out, b_down,
+                     gain_attn, shift_attn, gain_ffn, shift_ffn)
+    fsdp, tensor = lax.axis_size("fsdp"), lax.axis_size("tensor")
+    i, j = lax.axis_index("fsdp"), lax.axis_index("tensor")
+    rows, model = tokens.shape
+    shard, columns = w_query.shape
+    width = 2 * columns
+    down = w_down.T
+    pack = jnp.stack([pairs(w_key, w_value), pairs(w_query, w_out.T), w_up[:, :width], w_up[:, width:], down[:, :width], down[:, width:]])
+
+    def placed(vector):
+        mine = jnp.tile(vector.astype(F32), fsdp).reshape(fsdp, -1)
+        mine = jnp.where(lax.broadcasted_iota(jnp.int32, mine.shape, 0) == i, mine, 0.0)
+        return mine.reshape(1, -1)
+
+    def spread(vector, second):
+        vector = placed(vector)
+        zero = jnp.zeros_like(vector)
+        return pairs(zero, vector) if second else pairs(vector, zero)
+
+    small = jnp.concatenate([jnp.concatenate([spread(b_value, True), spread(b_query, False)], 1), placed(b_up),
+                             *map(placed, (b_out, b_down, gain_attn, shift_attn, gain_ffn, shift_ffn))])
+    weights, smalls, x, cot_in = gather_all(fsdp, tensor, pack, small, tokens, cotangent)
+    weights = weights.reshape(6, tensor, model, width)
+    w_kv, w_qo, up0, up1, dn0, dn1 = [weights[k] for k in range(6)]
+    smalls = jnp.sum(smalls, 1)
+    bias_kv, bias_q, bias_up = smalls[:, :1, :width], smalls[:, :1, width:], smalls[:, 1:2]
+    vecs = jnp.concatenate([smalls[0, 2:8], jnp.zeros((2, model), F32)])
+    half = tensor // 2
+    on = i % 2 == j // half
+    block = jnp.where(on, j, (j + half) % tensor)
+    x_own = lax.dynamic_index_in_dim(x, block, 0, False)
+    cot = jnp.where(on, cotangent, cot_in)
+    x_all = x.reshape(tensor * rows, model)
+    kv, q, att, inv, exps = attend(x_all, x_own, w_kv, w_qo, bias_kv, bias_q)
+    out, resid, datt, g_o, g_up0, g_up1, g_dn0, g_dn1, g_bup, g_vecs = feed_forward(
+        x_own, cot, att, w_qo, (up0, up1), (dn0, dn1), bias_up, vecs)
+    dx, dx_own, g_kv, g_qo, g_bkv, g_bq = backward(x_all, x_own, w_kv, w_qo, kv, q, att, inv, datt, g_o, exps)
+    tiny = jnp.concatenate([g_vecs, g_bup[:, 0], jnp.concatenate([g_bkv[:, 0], g_bq[:, 0]], 1)])
+    grads = [g.reshape(tensor, fsdp, shard, width) for g in (g_kv, g_qo, g_up0, g_up1, g_dn0, g_dn1)]
+    shards, grad_tokens, output, tiny = reduce_all(fsdp, tensor, grads, dx, resid, dx_own, out, tiny)
+
+    def apart(shard_pair):
+        both = shard_pair.reshape(shard, -1, 2, HEAD)
+        return both[:, :, 0].reshape(shard, columns), both[:, :, 1].reshape(shard, columns)
+
+    g_key, g_value = apart(shards[0])
+    g_query, g_out = apart(shards[1])
+    g_up = jnp.concatenate([shards[2], shards[3]], 1)
+    g_down = jnp.concatenate([shards[4], shards[5]], 1).T
+    mine = lambda vector, n: lax.dynamic_slice_in_dim(vector, i * n, n)
+    pick = lambda first: lax.dynamic_index_in_dim(tiny, first + j, 0, False)
+    both = pick(8 + tensor).reshape(2, -1, 2, HEAD)
+    g_bq, g_bv = both[1, :, 0].reshape(-1), both[0, :, 1].reshape(-1)
+    vectors = [mine(tiny[k], shard) for k in range(6)]
+    return (output, grad_tokens, g_query, g_key, g_value, g_out.T, g_up, g_down,
+            mine(g_bq, columns // fsdp), mine(g_bv, columns // fsdp), mine(pick(8), 2 * width // fsdp), *vectors)
+
+
 def solution(mesh):
     return jax.shard_map(
-        local,
+        layer,
         mesh=mesh,
         in_specs=(
             P(("fsdp", "tensor"), None),

time: 977 us -> 427 us (0.44)
  waiting for transfers between devices: 554 us -> 0 us
  Pallas kernels: 0 us -> 379 us
  matrix products: 186 us -> 0 us
  blocking collectives: 105 us -> 0 us
  other arithmetic: 63.6 us -> 10.1 us
  between operations: 19.5 us -> 0.97 us
    pallas_call x0 -> x5, Pallas kernels: none -> 379 us  [the longest x1 119 us: reduce_all(): pl.pallas_call(functools.partial(reduce_kernel, fsdp, tensor, chunks), in...]
    reduce_scatter x6 -> x0, waiting for transfers between devices: 243 us -> none  [the longest x1 59.5 us: local(): lax.psum_scatter(jnp.dot(attended, out_weight, preferred_element_type=jnp...]
    all_gather x6 -> x0, waiting for transfers between devices: 193 us -> none  [the longest x1 63.5 us: local(): lax.all_gather(grad_resid_attn.astype(jnp.bfloat16), 'tensor', axis=0, ti...]
    dot_general x45 -> x0, matrix products: 182 us -> none  [the longest x8 34.3 us: scores_of(): jnp.einsum('qhd,khd->hqk', piece, key_heads, preferred_element_type=jnp.f...]
    unnamed x20 -> x0, waiting for transfers between devices: 118 us -> none
    unnamed x3 -> x0, blocking collectives: 68.6 us -> none
    all_gather x4 -> x0, blocking collectives: 36.5 us -> none  [the longest x1 10 us: local(): lax.all_gather(w_query, 'fsdp', axis=0, tiled=True)]
    reduce_sum x17 -> x1, other arithmetic: 28.7 us -> 0.04 us  [layer(): smalls = jnp.sum(smalls, 1)]
  transfers between devices with their start and end apart: 16 -> 0, of which waited for: 12 -> 0; matrix products, arithmetic and copies ran while one was open for 21% -> 0% of each run, Pallas kernels for 0% -> 0%
where the time goes in v1:
time: 427 us; the launch traced here: 426 us
  Pallas kernels  379 us (89%)
  local copies, waits for them, and re-layouts  36.6 us (9%)
  other arithmetic  10.1 us (2%)
    pallas_call x1, Pallas kernels, reduce_all(): pl.pallas_call(functools.partial(reduce_kernel, fsdp, tensor, chunks), in...  119 us
    pallas_call x1, Pallas kernels, gather_all(): pl.pallas_call(functools.partial(gather_kernel, fsdp, tensor), in_specs=[...  116 us
    pallas_call x1, Pallas kernels, backward(): pl.pallas_call(functools.partial(backward_kernel, groups, heads, blocks),...  62.9 us
    pallas_call x1, Pallas kernels, feed_forward(): pl.pallas_call(functools.partial(ffn_kernel, groups), in_specs=[vm] * 10,...  43.3 us
    pallas_call x1, Pallas kernels, attend(): pl.pallas_call(functools.partial(attend_kernel, heads), grid=(groups,), i...  38.1 us
    slice x1, local copies, waits for them, and re-layouts, layer(): w_kv, w_qo, up0, up1, dn0, dn1 = [weights[k] for k in range(6)]  10.6 us
    unnamed x31, local copies, waits for them, and re-layouts  10.6 us

profile of v1, /device:TPU:0, one launch (start us, length us, event | category | flops | bytes accessed | tf_op | source)
XLA Modules:
  0.0 426.5 jit_solution(11776969327456582091)
XLA Ops:
  0.7 0.7 convert_element_type.27
  1.4 0.7 convert_element_type.28
  2.5 0.7 convert_element_type.29
  3.1 0.7 convert_element_type.30
  3.8 0.7 convert_element_type.31
  8.4 0.9 copy.39
  9.3 0.9 copy.40
  10.4 0.9 copy.42
  11.3 0.8 pad_maximum_fusion.2
  12.3 0.9 bitcast_dynamic-update-slice_fusion.1
  13.2 0.9 bitcast_dynamic-update-slice_fusion
  14.2 0.8 copy-done.4
  14.9 115.6 %shard_map.296 = (bf16[6,4,8,96,384]{4,3,2,1,0:T(8,128)(2,1)}, f32[4,8,8,768]{3,2,1,0:T(8,128)}, bf16[4,512,768]{2,1,0:T(8,128)(2,1)}, bf16[512,768]{1,0:T(8,128)(2,1)}) custom-call(bf16[6,96,384]{2,1,0:T(8,128)(2,1)} %copy-done.4, f32[8,768]{1,0:T(8,128)} %concatenate.22.small, bf16[512,768]{1,0:T(8,128)(2,1)} %tok.1, bf16[512,768]{1,0:T(8,128)(2,1)} %cot.1), custom_call_target="tpu_custom_call" | custom-call | tf_op jit(solution)/shard_map/pallas_call | solution.py:470
  130.5 2.1 dynamic-slice_bitcast_fusion.x_own
  132.6 10.6 %fusion.8 = (bf16[1,4,8,96,384]{4,3,2,1,0:T(8,128)(2,1)}, bf16[1,4,8,96,384]{4,3,2,1,0:T(8,128)(2,1)}, bf16[1,4,8,96,384]{4,3,2,1,0:T(8,128)(2,1)}, bf16[1,4,8,9...) fusion(bf16[6,4,8,96,384]{4,3,2,1,0:T(8,128)(2,1)} %get-tuple-element.47), kind=kLoop, calls=%fused_computation.50 | loop fusion | bytes 28311552 | tf_op jit(solution)/shard_map/slice | solution.py:981
  143.9 38.1 %shard_map.297 = (bf16[4,2048,384]{2,1,0:T(8,128)(2,1)}, bf16[4,512,384]{2,1,0:T(8,128)(2,1)}, bf16[4,512,384]{2,1,0:T(8,128)(2,1)}, f32[4,8,512]{2,1,0:T(8,128)}, bf16[4,3,2048,512]{3,2,1,0:T(8,128)(2,1)}) custom-call(bf16[2048,768]{1,0:T(8,128)(2,1)} %bitcast.82, bf16[512,768]{1,0:T(8,128)(2,1)} %dynamic-slice_bitcast_fusion.x_own, ...), custom_call_target="tpu_custom_call" | custom-call | tf_op jit(solution)/shard_map/pallas_call | solution.py:60
  181.9 1.0 broadcast_select_fusion.cot
  184.2 43.3 %shard_map.298 = (f32[512,768]{1,0:T(8,128)}, f32[512,768]{1,0:T(8,128)}, bf16[4,512,384]{2,1,0:T(8,128)(2,1)}, bf16[4,768,384]{2,1,0:T(8,128)(2,1)}, bf16[4,768...) custom-call(bf16[512,768]{1,0:T(8,128)(2,1)} %dynamic-slice_bitcast_, ...), custom_call_target="tpu_custom_call" | custom-call | tf_op jit(solution)/shard_map/pallas_call | solution.py:153
  227.5 62.9 %shard_map.299 = (bf16[4,512,768]{2,1,0:T(8,128)(2,1)}, f32[512,768]{1,0:T(8,128)}, bf16[4,768,384]{2,1,0:T(8,128)(2,1)}, bf16[4,768,384]{2,1,0:T(8,128)(2,1)}, ...) custom-call(bf16[2048,768]{1,0:T(8,128)(2,1)} %bitcast.83, bf16[512,768]{1,0:T(8,128)(2,1)} %dynamic-slice_bitcast_fusion.x_own, ...), custom_call_target="tpu_custom_call" | custom-call | tf_op jit(solution)/shard_map/pallas_call | solution.py:225
  290.4 0.7 copy_bitcast_fusion.1
  291.7 119.1 %shard_map.300 = (f32[6,96,384]{2,1,0:T(8,128)}, f32[512,768]{1,0:T(8,128)}, f32[512,768]{1,0:T(8,128)}, f32[16,768]{1,0:T(8,128)}) custom-call(bf16[4,8,96,384]{3,2,1,0:T(8,128)(2,1)} %bitcast.92, bf16[4,8,96,384]{3,2,1,0:T(8,128)(2,1)} %bitcast.93, bf16[4,8,96,384]{3,2,1,0:T(8,128)(2,1)} %bitcast.88, bf16[4,8,96,384]{3,2,1,0:T(8,128)(2,1)} %bitcast.89, ...), custom_call_target="tpu_custom_call" | custom-call | tf_op jit(solution)/shard_map/pallas_call | solution.py:670
  410.8 1.4 slice_bitcast_fusion.1
  412.2 0.7 maximum_bitcast_fusion
  413.0 0.7 pad_maximum_fusion
  413.8 0.7 fusion.9
  414.5 0.7 copy.48
  415.4 0.7 copy.49
  416.1 0.7 copy.50
  416.9 1.1 fusion.12
  422.9 1.3 dynamic-slice_bitcast_fusion.1
  424.2 1.1 copy.65
  425.3 1.1 copy.66
  (68 shorter events, 12.4 us)
Async XLA Ops:
  0.7 13.4 %copy-start.5 = (bf16[768,96]{0,1:T(8,128)(2,1)S(1)}, bf16[768,96]{0,1:T(8,128)(2,1)}, u32[]{:S(2)}) copy-start(bf16[768,96]{0,1:T(8,128)(2,1)} %param.24) | copy-start | bytes 442372
  14.1 0.8 copy-start.4
  132.6 10.6 %copy-start.3 = (f32[4,8,8,768]{3,2,1,0:T(8,128)S(1)}, f32[4,8,8,768]{3,2,1,0:T(8,128)}, u32[]{:S(2)}) copy-start(f32[4,8,8,768]{3,2,1,0:T(8,128)} %get-tuple-element.48) | copy-start | bytes 2359300
  143.9 38.1 %copy-start = (bf16[512,768]{1,0:T(8,128)(2,1)S(1)}, bf16[512,768]{1,0:T(8,128)(2,1)}, u32[]{:S(2)}) copy-start(bf16[512,768]{1,0:T(8,128)(2,1)} %cot.1) | copy-start | bytes 2359300
  227.4 63.6 %copy-start.7 = (f32[4,1,768]{2,1,0:T(1,128)S(1)}, f32[4,1,768]{2,1,0:T(1,128)}, u32[]{:S(2)}) copy-start(f32[4,1,768]{2,1,0:T(1,128)} %get-tuple-element.68) | copy-start | bytes 36868
  227.5 63.6 %copy-start.6 = (f32[8,768]{1,0:T(8,128)S(1)}, f32[8,768]{1,0:T(8,128)}, u32[]{:S(2)}) copy-start(f32[8,768]{1,0:T(8,128)} %get-tuple-element.67) | copy-start | bytes 73732
  410.8 13.4 %copy-start.2 = (f32[512,768]{1,0:T(8,128)S(1)}, f32[512,768]{1,0:T(8,128)}, u32[]{:S(2)}) copy-start(f32[512,768]{1,0:T(8,128)} %get-tuple-element.147) | copy-start | bytes 4718596
  414.5 10.8 %copy-start.1 = (f32[512,768]{1,0:T(8,128)S(1)}, f32[512,768]{1,0:T(8,128)}, u32[]{:S(2)}) copy-start(f32[512,768]{1,0:T(8,128)} %get-tuple-element.148) | copy-start | bytes 4718596

commit v2 on v0

--- a/solution.py
+++ b/solution.py
@@ -1,14 +1,952 @@
+import functools
+
 import jax
 import jax.numpy as jnp
+import numpy as np
 from jax import lax
+from jax.experimental import pallas as pl
+from jax.experimental.pallas import tpu as pltpu
 from jax.sharding import PartitionSpec as P
 
+F32, BF16 = jnp.float32, jnp.bfloat16
 HEAD = 64
-
-
 EPSILON = 1e-12
-CONTRACT_LAST = (((1,), (1,)), ((), ()))
-CONTRACT_FIRST = (((0,), (0,)), ((), ()))
+VMEM_LIMIT = 64000 * 1024
+
+
+def dot(left, right, contract):
+    return lax.dot_general(left, right, ((contract[:1], contract[1:]), ((), ())), preferred_element_type=F32)
+
+NN, NT, TN = (1, 0), (1, 1), (0, 0)
+
+
+def lanes_from(shape, low):
+    return lax.broadcasted_iota(jnp.int32, shape, len(shape) - 1) % (2 * HEAD) >= HEAD if not low else \
+        lax.broadcasted_iota(jnp.int32, shape, len(shape) - 1) % (2 * HEAD) < HEAD
+
+
+def project_keys(x, w, bias):
+    return (dot(x, w, NN) + bias).astype(BF16)
+
+
+def project_query(x, w, bias):
+    out = dot(x, w, NN) + bias
+    return jnp.where(lanes_from(out.shape, True), out.astype(BF16) * BF16(HEAD ** -0.5), BF16(0))
+
+
+def norm_forward(z):
+    mean = jnp.mean(z, -1, keepdims=True)
+    centered = z - mean
+    inv = lax.rsqrt(jnp.mean(centered * centered, -1, keepdims=True) + EPSILON)
+    return centered * inv, inv
+
+
+def norm_backward(n, inv, dn):
+    return inv * (dn - jnp.mean(dn, -1, keepdims=True) - n * jnp.mean(dn * n, -1, keepdims=True))
+
+
+def colsum(x):
+    return jnp.sum(x.astype(F32), axis=0, keepdims=True)
+
+
+MESH = pl.DeviceIdType.MESH
+ANY = pl.BlockSpec(memory_space=pl.ANY)
+VM = pl.BlockSpec(memory_space=pltpu.VMEM)
+
+
+def flip(index, bit):
+    return index + bit - 2 * bit * lax.rem(index // bit, 2)
+
+
+def flips(index, mask):
+    bit = 1
+    while bit <= mask:
+        if mask & bit:
+            index = flip(index, bit)
+        bit *= 2
+    return index
+
+
+def span(bits):
+    masks = [0]
+    for bit in bits:
+        masks += [m | bit for m in masks]
+    return masks
+
+
+def orders(fsdp):
+    bits = [1 << k for k in range(fsdp.bit_length() - 1)]
+    return bits[1:] + bits[:1], bits[:0:-1] + bits[:1]
+
+
+class Place:
+    def __init__(self, fsdp, tensor):
+        self.fsdp, self.tensor = fsdp, tensor
+        self.i, self.j = lax.axis_index("fsdp"), lax.axis_index("tensor")
+        self.half = tensor // 2
+        self.c = lax.rem(self.i, 2)
+        self.h = self.j // self.half
+        self.on = self.c == self.h
+        self.off = self.c != self.h
+        self.twin = flip(self.i, 1)
+        self.swap = lax.rem(self.j + self.half, tensor)
+        self.block = jnp.where(self.on, self.j, self.swap)
+        self.edge = self.half - 1 + self.c
+        self.end = self.c * (tensor - 1)
+        self.mate = self.h * tensor + 1 - self.j
+        self.is_edge = self.j == self.edge
+        self.is_end = self.j == self.end
+
+    def other(self, k):
+        return (1 - self.c) * (self.half + k) + self.c * (self.half - 1 - k)
+
+    def near(self, n):
+        low = jnp.where(self.h == 0, self.j, self.tensor - 1 - self.j)
+        if isinstance(n, int):
+            place = low if n == 0 else 1 - low if n == 1 else n
+        else:
+            place = jnp.where(n == 0, low, jnp.where(n == 1, 1 - low, n))
+        return jnp.where(self.h == 0, place, self.tensor - 1 - place)
+
+    def barrier(self):
+        sem = pltpu.get_barrier_semaphore()
+        others = [(self.i, lax.rem(self.j + k, self.tensor)) for k in range(1, self.tensor)]
+        bit = 1
+        while bit < self.fsdp:
+            others.append((flip(self.i, bit), self.j))
+            bit *= 2
+        others.append((self.twin, self.swap))
+        for i, j in others:
+            pl.semaphore_signal(sem, inc=1, device_id=(i, j), device_id_type=MESH)
+        pl.semaphore_wait(sem, len(others))
+
+
+class Sends:
+    def __init__(self, place, send, recv):
+        self.place, self.send, self.recv, self.n, self.started = place, send, recv, 0, []
+
+    def slots(self, n):
+        self.n += n
+        return self.n - n
+
+    def slot(self):
+        return self.slots(1)
+
+    def copy(self, src, dst, slot, i, j, back=None):
+        return pltpu.make_async_remote_copy(src_ref=src, dst_ref=dst, send_sem=self.send.at[slot if back is None else back],
+                                            recv_sem=self.recv.at[slot], device_id=(i, j), device_id_type=MESH)
+
+    def start(self, src, dst, slot, i, j, when=None, back=None, note=True):
+        copy = self.copy(src, dst, slot, i, j, back)
+        copy.start() if when is None else pl.when(when)(copy.start)
+        if note:
+            self.started.append((copy, when))
+
+    def arrive(self, dst, slot, when=None):
+        copy = self.copy(dst, dst, slot, self.place.i, self.place.j)
+        copy.wait_recv() if when is None else pl.when(when)(copy.wait_recv)
+
+    def left(self, src, slot, when=None):
+        copy = self.copy(src, src, slot, self.place.i, self.place.j)
+        copy.wait_send() if when is None else pl.when(when)(copy.wait_send)
+
+    def finish(self):
+        for copy, when in self.started:
+            copy.wait_send() if when is None else pl.when(when)(copy.wait_send)
+        self.started = []
+
+
+class Stream:
+    def __init__(self, sends, array, lead, shard, order, own):
+        self.s, self.p, self.a, self.lead, self.shard, self.order, self.own = sends, sends.place, array, lead, shard, order, own
+        n = self.p.tensor
+        self.z, self.back = sends.slots(n), sends.slots(1)
+        self.hops = [{m: sends.slots(n) for m in span(order[:k])} for k in range(len(order))]
+
+    def block(self, t, mask):
+        rows = pl.ds(pl.multiple_of(flips(self.p.i, mask) * self.shard, self.shard), self.shard)
+        return self.a.at[(*self.lead, t, rows)]
+
+    def first_line(self):
+        s, p = self.s, self.p
+        there = self.block(p.j, 0)
+        s.start(self.own, there, self.z + p.j, p.i, p.j + 1, p.j + 1 < p.tensor, note=False)
+        s.start(self.own, there, self.z + p.j, p.i, p.j - 1, p.j > 0, self.back, note=False)
+
+    def first_fan(self):
+        self.fan(0, 0, self.p.j, self.own)
+
+    def fan(self, mask, k, t, src=None):
+        for n in range(k, len(self.order)):
+            there = self.block(t, mask)
+            self.s.start(there if src is None else src, there, self.hops[n][mask] + t, flip(self.p.i, self.order[n]), self.p.j, note=False)
+
+    def line(self, n):
+        s, p = self.s, self.p
+        t = p.near(n)
+        there = self.block(t, 0)
+        s.arrive(there, self.z + t)
+        ahead = p.j + jnp.where(t < p.j, 1, -1)
+        s.start(there, there, self.z + t, p.i, ahead, (ahead >= 0) & (ahead < p.tensor), note=False)
+        self.fan(0, 0, t)
+
+    def finish(self):
+        s, p = self.s, self.p
+        here = self.block(p.j, 0)
+        s.left(here, self.z + p.j, p.j + 1 < p.tensor)
+        s.left(here, self.back, p.j > 0)
+        for n in range(p.tensor):
+            t = p.near(n)
+            if n > 0:
+                ahead = p.j + jnp.where(t < p.j, 1, -1)
+                s.left(here, self.z + t, (ahead >= 0) & (ahead < p.tensor))
+            for hops in self.hops:
+                for slot in hops.values():
+                    s.left(here, slot + t)
+
+    def hop(self, k, n):
+        t = self.p.near(n)
+        for m in self.hops[k]:
+            mask = m | self.order[k]
+            self.s.arrive(self.block(t, mask), self.hops[k][m] + t)
+            self.fan(mask, k + 1, t)
+
+
+def attend_group(heads, g, x, own_rows, w_kv, w_qo, smalls, kv, q, att, inv, s_ref, exps, before, after):
+    width = heads * 128
+    kv[g] = project_keys(x[...], w_kv[g], smalls[g, 0:1, :width])
+    q[g] = project_query(x[own_rows, :], w_qo[g], smalls[g, 0:1, width:])
+    for h in range(heads):
+        cols = slice(h * 128, h * 128 + 128)
+        keys = kv[g, :, cols]
+        s_ref[...] = dot(keys, q[g, :, cols], NT)
+        top = jnp.max(s_ref[...], axis=0, keepdims=True)
+        e = jnp.exp(s_ref[...] - top)
+        scale = 1.0 / jnp.sum(e, axis=0, keepdims=True)
+        before(h)
+        exps[h] = e.astype(BF16)
+        out = dot(keys, exps[h], TN) * scale
+        out = jnp.where(lax.broadcasted_iota(jnp.int32, out.shape, 0) >= HEAD, out, 0.0)
+        att[g, :, cols] = out.T.astype(BF16)
+        inv[g, h:h + 1] = scale
+        after(h)
+
+
+def first_kernel(fsdp, tensor, pack, small, tok, cot, w0_out, w1, x_out, own_out, cot_out, kv_out, q_out, att_out, exp_out,
+                 inv, smalls, w0, sm, x, kv, q, att, s_ref, exps, send, recv, local):
+    p = Place(fsdp, tensor)
+    s = Sends(p, send, recv)
+    rows, model = tok.shape
+    shard = pack.shape[1]
+    heads = exps.shape[0]
+    first, second = orders(fsdp)
+    kvw = Stream(s, w0, (0,), shard, first, pack.at[0])
+    qow = Stream(s, w0, (1,), shard, second, pack.at[1])
+    tiny = Stream(s, sm, (), small.shape[0], first, small)
+    upper = Stream(s, w1, (pl.ds(0, 2),), shard, first, pack.at[pl.ds(2, 2)])
+    lower = Stream(s, w1, (pl.ds(2, 2),), shard, second, pack.at[pl.ds(4, 2)])
+    now, later = (kvw, qow, tiny), (upper, lower)
+    pieces = 4 if rows % 64 == 0 else 1
+    part = rows // pieces
+    xin, xtwin, cslot = s.slots(tensor * pieces), s.slots(tensor * pieces), s.slots(1)
+    x_at = lambda t: x.at[pl.ds(pl.multiple_of(t * rows, rows), rows)]
+
+    def piece(t, u):
+        return x.at[pl.ds(pl.multiple_of(t * rows + u * part, part), part)]
+
+    def send_rows(t, u, i, j, when, twin=False, src=None):
+        slot = t * pieces + u
+        there = piece(t, u)
+        s.start(there if src is None else src.at[pl.ds(u * part, part)], there, xin + slot, i, j, when, xtwin + slot if twin else None)
+
+    def pass_rows(u, n, when, forward):
+        t = p.near(n)
+        s.arrive(piece(t, u), xin + t * pieces + u, when)
+        if forward:
+            send_rows(t, u, p.i, p.end, when)
+        send_rows(t, u, p.twin, p.j, when, True)
+
+    def edge_rows(u):
+        for n in [*range(2, tensor), 1]:
+            pass_rows(u, n, p.on & p.is_edge, p.half > 1 and n > 1)
+
+    def end_rows(u):
+        for n in range(1, tensor):
+            pass_rows(u, n, p.on & jnp.logical_not(p.is_edge), False)
+    locals_ = []
+
+    def keep(src, dst, when=None):
+        copy = pltpu.make_async_copy(src, dst, local.at[len(locals_)])
+        copy.start() if when is None else pl.when(when)(copy.start)
+        locals_.append((copy, when))
+        return len(locals_) - 1
+
+    def kept(k):
+        copy, when = locals_[k]
+        copy.wait() if when is None else pl.when(when)(copy.wait)
+        locals_[k] = None
+
+    mine = pl.ds(pl.multiple_of(p.i * shard, shard), shard)
+    own = [keep(pack.at[k], w0.at[k, p.j, mine]) for k in range(2)]
+    own += [keep(pack.at[2 + k], w1.at[k, p.j, mine]) for k in range(4)]
+    own += [keep(small, sm.at[p.j, pl.ds(pl.multiple_of(p.i * small.shape[0], small.shape[0]), small.shape[0])])]
+    own += [keep(tok, x_at(p.j), p.on), keep(cot, cot_out, p.on)]
+    p.barrier()
+    for g in now:
+        g.first_line()
+    for g in now:
+        g.first_fan()
+    for u in range(pieces):
+        send_rows(p.j, u, p.i, p.edge, p.off, src=tok)
+        if p.half > 1:
+            send_rows(p.j, u, p.i, p.mate, p.on, src=tok)
+        send_rows(p.j, u, p.twin, p.j, p.on, True, tok)
+    for g in later:
+        g.first_fan()
+    stages = len(first)
+    for step in range(1, tensor + stages - 1):
+        if step < tensor:
+            for g in now:
+                g.line(step)
+        for k in range(stages - 1):
+            if 0 <= step - 1 - k < tensor:
+                for g in now:
+                    g.hop(k, step - 1 - k)
+        if step - 1 < pieces:
+            edge_rows(step - 1)
+    for u in range(tensor + stages - 2, pieces):
+        edge_rows(u)
+    for u in range(pieces):
+        end_rows(u)
+    for g in later:
+        g.first_line()
+    for k in range(stages - 1):
+        for g in later:
+            g.hop(k, 0)
+    s.start(cot, cot_out, cslot, p.twin, p.swap, p.off)
+    for n in range(tensor):
+        for g in now:
+            g.hop(stages - 1, n)
+    for t in range(tensor):
+        for u in range(pieces):
+            s.arrive(piece(t, u), xin + t * pieces + u, p.off)
+    for k in own[:8]:
+        kept(k)
+    for t in range(tensor):
+        total = sm[t, :small.shape[0], :]
+        for i in range(1, fsdp):
+            total += sm[t, i * small.shape[0]:(i + 1) * small.shape[0], :]
+        smalls[t] = total
+    keep(x_at(p.block), own_out)
+    for t in range(tensor):
+        keep(x_at(t), x_out.at[pl.ds(t * rows, rows)])
+    for k in range(2):
+        keep(w0.at[k], w0_out.at[k])
+    fixed = len(locals_)
+    sem = lambda k: local.at[fixed + k]
+
+    def group(g, carry):
+        def exp_copy(h, g):
+            return pltpu.make_async_copy(exps.at[h], exp_out.at[g, h], sem(h))
+
+        def before(h):
+            pl.when(g > 0)(lambda: exp_copy(h, g - 1).wait())
+
+        def after(h):
+            exp_copy(h, g).start()
+            point = {0: 0, heads // 2: 1, heads - 1: 2}.get(h)
+            if point == 0:
+                @pl.when(g >= 2)
+                def _():
+                    for st in later:
+                        for k in range(1, stages - 1):
+                            st.hop(k, g - 1)
+            if point == 1:
+                @pl.when(g >= 1)
+                def _():
+                    for st in later:
+                        st.hop(0, g)
+            if point == 2:
+                @pl.when(g < tensor - 1)
+                def _():
+                    for st in later:
+                        st.line(g + 1)
+
+        attend_group(heads, g, x, pl.ds(pl.multiple_of(p.block * rows, rows), rows), w0.at[0], w0.at[1], smalls, kv, q, att, inv,
+                     s_ref, exps, before, after)
+        for k, (src, dst) in enumerate(((kv, kv_out), (q, q_out), (att, att_out))):
+            pltpu.make_async_copy(src.at[g], dst.at[g], sem(heads + k * tensor + g)).start()
+        return carry
+
+    lax.fori_loop(0, tensor, group, 0)
+    for k in range(1, stages - 1):
+        for st in later:
+            st.hop(k, tensor - 1)
+    for n in range(tensor):
+        for st in later:
+            st.hop(stages - 1, n)
+    for h in range(heads):
+        pltpu.make_async_copy(exps.at[h], exp_out.at[0, h], sem(h)).wait()
+    for k, (src, dst) in enumerate(((kv, kv_out), (q, q_out), (att, att_out))):
+        for g in range(tensor):
+            pltpu.make_async_copy(src.at[g], dst.at[g], sem(heads + k * tensor + g)).wait()
+    s.arrive(cot_out, cslot, p.off)
+    for k in range(len(locals_)):
+        if locals_[k] is not None:
+            kept(k)
+    s.finish()
+    for st in now + later:
+        st.finish()
+
+
+def first_part(fsdp, tensor, pack, small, tok, cot):
+    chunks, shard, width = pack.shape
+    rows, model = tok.shape
+    heads, keys = width // 128, tensor * rows
+    slots = 5 * (tensor + 1 + (fsdp - 1) * tensor) + 8 * tensor + 1
+    return pl.pallas_call(
+        functools.partial(first_kernel, fsdp, tensor),
+        in_specs=[VM] * 4, out_specs=[ANY] * 9 + [VM] * 2,
+        out_shape=[jax.ShapeDtypeStruct(s, d) for s, d in [
+            ((2, tensor, model, width), BF16), ((4, tensor, model, width), BF16), ((keys, model), BF16), ((rows, model), BF16),
+            ((rows, model), BF16), ((tensor, keys, width), BF16), ((tensor, rows, width), BF16), ((tensor, rows, width), BF16),
+            ((tensor, heads, keys, rows), BF16), ((tensor, 8, rows), F32), ((tensor, *small.shape), F32)]],
+        scratch_shapes=[pltpu.VMEM(s, d) for s, d in [
+            ((2, tensor, model, width), BF16), ((tensor, fsdp * small.shape[0], model), F32), ((keys, model), BF16),
+            ((tensor, keys, width), BF16), ((tensor, rows, width), BF16), ((tensor, rows, width), BF16), ((keys, rows), F32),
+            ((heads, keys, rows), BF16)]] + [pltpu.SemaphoreType.DMA((slots,)), pltpu.SemaphoreType.DMA((slots,)),
+                                             pltpu.SemaphoreType.DMA((16 + 5 * tensor + heads,))],
+        compiler_params=pltpu.CompilerParams(collective_id=0, has_side_effects=True, vmem_limit_bytes=VMEM_LIMIT),
+    )(pack, small, tok, cot)
+
+
+class Loads:
+    def __init__(self, sems):
+        self.sems, self.n = sems, 0
+
+    def slots(self, n):
+        self.n += n
+        return self.n - n
+
+    def load(self, src, dst):
+        copy = pltpu.make_async_copy(src, dst, self.sems.at[self.slots(1)])
+        copy.start()
+        return copy
+
+    def series(self, src, dst, n):
+        first = self.slots(n)
+        for k in range(n):
+            pltpu.make_async_copy(src.at[k], dst.at[k], self.sems.at[first + k]).start()
+        return lambda k: pltpu.make_async_copy(src.at[k], dst.at[k], self.sems.at[first + k]).wait()
+
+
+def middle_kernel(groups, x_hbm, cot_hbm, att_hbm, w0_hbm, w1_hbm, smalls, inv,
+                  out_ref, out_low, resid_ref, r_ref, datt_hbm, g_o_hbm, g_hbm, g_bup, g_vecs,
+                  x_own, cot, att, w_qo, w1, datt, g_o, grads, act, slope, hid, n1_ref, acc, low, hl, sems):
+    ld = Loads(sems)
+    width = w_qo.shape[2]
+    get_x = ld.load(x_hbm, x_own)
+    get_att = ld.series(att_hbm, att, groups)
+    get_qo = ld.series(w0_hbm.at[1], w_qo, groups)
+    gets = [ld.series(w1_hbm.at[k], w1.at[k], groups) for k in range(4)]
+    get_cot = ld.load(cot_hbm, cot)
+    outs = [(grads.at[k], g_hbm.at[k], ld.slots(groups)) for k in range(4)]
+    outs += [(datt, datt_hbm, ld.slots(groups)), (g_o, g_o_hbm, ld.slots(groups))]
+
+    def put(k, g):
+        src, dst, first = outs[k]
+        return pltpu.make_async_copy(src.at[g], dst.at[g], sems.at[first + g])
+
+    vec = lambda k: smalls[0, 2 + k:3 + k, :]
+    get_x.wait()
+    acc[...] = x_own[...].astype(F32) + vec(0)
+
+    def branch(g, c):
+        get_att(g)
+        get_qo(g)
+        acc[...] += dot(att[g], w_qo[g], NT)
+        return c
+
+    lax.fori_loop(0, groups, branch, 0)
+    n1, inv1 = norm_forward(acc[...])
+    n1_ref[...] = n1
+    hidden = n1 * vec(2) + vec(3)
+    hid[...] = hidden
+    hl[...] = hidden.astype(BF16)
+    acc[...] = hidden + vec(1)
+
+    def forward(g, c):
+        for k in range(2):
+            gets[2 * k](g)
+            gets[2 * k + 1](g)
+            pre = dot(hl[...], w1[2 * k, g], NN) + smalls[g, 1:2, k * width:(k + 1) * width]
+            phi = 0.5 + 0.5 * lax.erf(pre * np.float32(0.5 ** 0.5))
+            slope[g, k] = phi + pre * (jnp.exp(-0.5 * pre * pre) * np.float32((2 * np.pi) ** -0.5))
+            act[g, k] = (pre * phi).astype(BF16)
+            acc[...] += dot(act[g, k], w1[2 * k + 1, g], NT)
+        return c
+
+    lax.fori_loop(0, groups, forward, 0)
+    n2, inv2 = norm_forward(acc[...])
+    out = n2 * vec(4) + vec(5)
+    out_ref[...] = out
+    out_low[...] = out.astype(BF16)
+    get_cot.wait()
+    cott = cot[...].astype(F32)
+    g_vecs[4:5] = colsum(cott * n2)
+    g_vecs[5:6] = colsum(cott)
+    resid = norm_backward(n2, inv2, cott * vec(4))
+    acc[...] = resid
+    low[...] = resid.astype(BF16)
+    g_vecs[1:2] = colsum(low[...])
+
+    def back(g, c):
+        for k in range(2):
+            grads[2 * k + 1, g] = dot(low[...], act[g, k], TN).astype(BF16)
+            put(2 * k + 1, g).start()
+            gp = (dot(low[...], w1[2 * k + 1, g], NN) * slope[g, k]).astype(BF16)
+            act[g, k] = gp
+            g_bup[g, :, k * width:(k + 1) * width] = colsum(gp)
+            grads[2 * k, g] = dot(hl[...], gp, TN).astype(BF16)
+            put(2 * k, g).start()
+            acc[...] += dot(act[g, k], w1[2 * k, g], NT)
+        return c
+
+    lax.fori_loop(0, groups, back, 0)
+    gh = acc[...]
+    g_vecs[2:3] = colsum(gh * n1_ref[...])
+    g_vecs[3:4] = colsum(gh)
+    ga = norm_backward(n1_ref[...], inv1, gh * vec(2))
+    resid_ref[...] = ga
+    low[...] = ga.astype(BF16)
+    g_vecs[0:1] = colsum(low[...])
+    g_vecs[6:8] = jnp.zeros_like(g_vecs[6:8])
+
+    def last(g, c):
+        da = dot(low[...], w_qo[g], NN)
+        da = jnp.where(lanes_from(da.shape, False), da, 0.0).T.astype(BF16).astype(F32)
+        prod = da * att[g].T.astype(F32)
+        for h in range(width // 128):
+            cols = slice(h * 128, h * 128 + 128)
+            scale = inv[g, h:h + 1]
+            r_ref[g, h:h + 1] = jnp.sum(prod[cols], axis=0, keepdims=True) * scale
+            datt[g, :, cols] = (da[cols] * scale).T.astype(BF16)
+        put(4, g).start()
+        g_o[g] = dot(low[...], att[g], TN).astype(BF16)
+        put(5, g).start()
+        return c
+
+    lax.fori_loop(0, groups, last, 0)
+    for k in range(6):
+        for g in range(groups):
+            put(k, g).wait()
+
+
+def middle_part(x_own, cot, att, w0, w1, smalls, inv):
+    _, groups, model, width = w0.shape
+    rows = x_own.shape[0]
+    wide, deep = ((groups, rows, width), BF16), ((groups, model, width), BF16)
+    flat, low = ((rows, model), F32), ((rows, model), BF16)
+    return pl.pallas_call(
+        functools.partial(middle_kernel, groups),
+        in_specs=[ANY] * 5 + [VM] * 2, out_specs=[VM] * 4 + [ANY, ANY, ANY, VM, VM],
+        out_shape=[jax.ShapeDtypeStruct(s, d) for s, d in [
+            flat, low, flat, ((groups, 8, rows), F32), wide, deep, ((4, groups, model, width), BF16), ((groups, 1, 2 * width), F32), ((8, model), F32)]],
+        scratch_shapes=[pltpu.VMEM(s, d) for s, d in [
+            low, low, wide, deep, ((4, groups, model, width), BF16), wide, deep, ((4, groups, model, width), BF16),
+            ((groups, 2, rows, width), BF16), ((groups, 2, rows, width), F32), flat, flat, flat, low, low]]
+        + [pltpu.SemaphoreType.DMA((12 * groups + 2,))],
+        compiler_params=pltpu.CompilerParams(vmem_limit_bytes=VMEM_LIMIT),
+    )(x_own, cot, att, w0, w1, smalls, inv)
+
+
+class Fold:
+    def __init__(self, sends, give, keep, lead, halves, inbox, order, out):
+        self.s, self.p, self.give, self.keep, self.lead = sends, sends.place, give, keep, lead
+        self.halves, self.inbox, self.order, self.out = halves, inbox, order[::-1], out
+        n = self.p.tensor
+        self.masks = [span(self.order[k + 1:]) for k in range(len(order))]
+        self.slot = [[sends.slots(n) for _ in masks] for masks in self.masks]
+        self.z = sends.slots(2 * n)
+
+    def half(self, k, mask, t):
+        return self.halves[k].at[(self.lead, self.masks[k].index(mask), t)]
+
+    def first(self, n):
+        t, bit = self.p.near(n), self.order[0]
+        for k, m in enumerate(self.masks[0]):
+            self.s.start(self.give(t, m | bit), self.half(0, m, t), self.slot[0][k] + t, flip(self.p.i, bit), self.p.j, note=False)
+
+    def add(self, k, n):
+        t = self.p.near(n)
+        for at, m in enumerate(self.masks[k]):
+            here = self.half(k, m, t)
+            self.s.arrive(here, self.slot[k][at] + t)
+            mine = self.keep(t, at) if k == 0 else self.half(k - 1, m, t)
+            here[...] = (here[...].astype(F32) + mine[...].astype(F32)).astype(BF16)
+        if k + 1 < len(self.order):
+            bit = self.order[k + 1]
+            for at, m in enumerate(self.masks[k + 1]):
+                self.s.start(self.half(k, m | bit, t), self.half(k + 1, m, t), self.slot[k + 1][at] + t,
+                             flip(self.p.i, bit), self.p.j, note=False)
+
+    def total(self, t):
+        return self.half(len(self.order) - 1, 0, t)
+
+    def way(self, n):
+        t = self.p.near(n)
+        right = t > self.p.j
+        there = self.p.j + jnp.where(right, 1, -1)
+        before = self.p.j - jnp.where(right, 1, -1)
+        side = jnp.where(right, 0, 1)
+        has = (before >= 0) & (before < self.p.tensor)
+        return t, there, has, self.inbox.at[(self.lead, side, t)], self.z + side * self.p.tensor + t
+
+    def line_first(self, n):
+        t, there, has, box, slot = self.way(n)
+        self.s.start(self.total(t), box, slot, self.p.i, there, jnp.logical_not(has), note=False)
+
+    def line_next(self, n):
+        t, there, has, box, slot = self.way(n)
+        total = self.total(t)
+
+        @pl.when(has)
+        def _():
+            self.s.arrive(box, slot)
+            box[...] = (box[...].astype(F32) + total[...].astype(F32)).astype(BF16)
+            self.s.start(box, box, slot, self.p.i, there, note=False)
+
+    def result(self):
+        p = self.p
+        self.out[...] = self.total(p.j)[...].astype(F32)
+        for side, there in ((0, p.j > 0), (1, p.j < p.tensor - 1)):
+            box = self.inbox.at[(self.lead, side, p.j)]
+
+            @pl.when(there)
+            def _(box=box, side=side):
+                self.s.arrive(box, self.z + side * p.tensor + p.j)
+                self.out[...] += box[...].astype(F32)
+
+    def finish(self):
+        here = self.half(0, self.masks[0][0], 0)
+        for n in range(self.p.tensor):
+            t = self.p.near(n)
+            for slots in self.slot:
+                for slot in slots:
+                    self.s.left(here, slot + t)
+            if n > 0:
+                self.s.left(here, self.way(n)[4])
+
+
+def last_kernel(fsdp, tensor, x_hbm, w0_hbm, kv_hbm, q_hbm, do_hbm, g_o_hbm, g_hbm, e_hbm, resid_hbm, low_hbm, r, g_bup, g_vecs,
+                shards, dx, tiny, swapped, *scratch):
+    bits = fsdp.bit_length() - 1
+    halves, scratch = scratch[:bits], scratch[bits:]
+    (inbox, own_g, x, w0, kv, q, do, dqt, wacc, exps, gw, dkv, dxb, own, twin_in, mate_in, fin_in, tiny_in, send, recv, local) = scratch
+    p = Place(fsdp, tensor)
+    s, ld = Sends(p, send, recv), Loads(local)
+    _, heads, rows, _ = exps.shape
+    model, width = gw.shape[2:]
+    shard = model // fsdp
+    first, second = orders(fsdp)
+    block_rows = lambda mask: pl.ds(pl.multiple_of(flips(p.i, mask) * shard, shard), shard)
+    pair = lambda k: pl.ds(2 * k, 2)
+    stay = [m for m in span(first[::-1][1:])]
+    folds = []
+    for k, order in enumerate((first, second)):
+        masks = span(order[::-1][1:])
+        folds.append(Fold(s, lambda t, m, k=k: g_hbm.at[pair(k), t, block_rows(m)],
+                          lambda t, at, k=k, masks=masks: own_g.at[pair(k), t, stay.index(masks[at])],
+                          pair(k + 1), halves, inbox, order, shards.at[pair(k + 1)]))
+    tails = []
+    for k, order in enumerate((first, second)):
+        masks = span(order[::-1][1:])
+        tails.append(Fold(s, lambda t, m, k=k: gw.at[pl.ds(k, 1), t, block_rows(m)],
+                          lambda t, at, k=k, masks=masks: gw.at[pl.ds(k, 1), t, block_rows(masks[at])],
+                          pl.ds(k, 1), halves, inbox, order, shards.at[pl.ds(k, 1)]))
+    stages = bits
+
+    steps = tensor * tensor
+    step_sem, x_sem = ld.slots(4), ld.slots(2)
+
+    def step_copies(step, slot):
+        t, g = p.near(tensor - 1 - step // tensor), p.near(tensor - 1 - lax.rem(step, tensor))
+        here = pl.ds(pl.multiple_of(t * rows, rows), rows)
+        return (pltpu.make_async_copy(e_hbm.at[g, :, here], exps.at[slot], local.at[step_sem + slot]),
+                pltpu.make_async_copy(kv_hbm.at[g, here], kv.at[slot], local.at[step_sem + 2 + slot]))
+
+    def x_copy(it, slot):
+        t = p.near(tensor - 1 - it)
+        return pltpu.make_async_copy(x_hbm.at[pl.ds(pl.multiple_of(t * rows, rows), rows)], x.at[slot], local.at[x_sem + slot])
+
+    for copy in step_copies(0, 0):
+        copy.start()
+    gets = [ld.load(do_hbm, do), ld.load(q_hbm, q)]
+    x_copy(0, 0).start()
+    gets.append(ld.load(w0_hbm, w0))
+    own_gets = [ld.load(g_hbm.at[:, :, block_rows(m)], own_g.at[:, :, at]) for at, m in enumerate(stay)]
+    gets.append(ld.load(g_o_hbm, gw.at[1]))
+    gets.append(ld.load(resid_hbm, own))
+    own_sem = ld.slots(1)
+    tiny[:8] = g_vecs[...]
+    for t in range(tensor):
+        tiny[8 + t:9 + t] = g_bup[t]
+    tiny[8 + tensor:] = jnp.zeros_like(tiny[8 + tensor:])
+    p.barrier()
+    for n in range(tensor)[::-1]:
+        for f in folds:
+            f.first(n)
+    swap_slot = s.slots(1)
+    s.start(low_hbm, swapped, swap_slot, p.twin, p.swap, p.off)
+    twin, mate, fin = s.slots(tensor), s.slots(tensor), s.slots(1)
+    fin_send, own_slot = s.slots(tensor), s.slots(1)
+    tiny_slots = s.slots((fsdp * tensor).bit_length() - 1)
+    wacc[...] = jnp.zeros_like(wacc)
+    dqt[...] = jnp.zeros_like(dqt)
+    for copy in gets + own_gets:
+        copy.wait()
+
+    def rows_to_twin(n, slot):
+        t = p.near(n)
+        s.start(dxb.at[slot], twin_in.at[t], twin + t, p.twin, p.j, p.off, note=False)
+
+    def rows_from_twin(n, slot):
+        t = p.near(n)
+
+        @pl.when(p.on)
+        def _():
+            s.arrive(twin_in.at[t], twin + t)
+            twin_in[t] = (twin_in[t].astype(F32) + dxb[slot].astype(F32)).astype(BF16)
+        if p.half > 1:
+            to_mate = p.on & ((n == 1) | ((n > 1) & p.is_end))
+            s.start(twin_in.at[t], mate_in.at[t], mate + t, p.i, p.mate, to_mate, note=False)
+        else:
+            s.start(twin_in.at[t], fin_in, fin, p.i, t, p.on, fin_send + t, note=False)
+
+    def rows_from_mate(n):
+        t = p.near(n)
+        here = p.on & p.is_edge
+
+        @pl.when(here)
+        def _():
+            s.arrive(mate_in.at[t], mate + t)
+            mate_in[t] = (mate_in[t].astype(F32) + twin_in[t].astype(F32)).astype(BF16)
+        s.start(mate_in.at[t], fin_in, fin, p.i, t, here, fin_send + t, note=False)
+
+    def one(it, gi):
+        n = tensor - 1 - it
+        t, g = p.near(n), p.near(tensor - 1 - gi)
+        step = it * tensor + gi
+        slot, x_slot = lax.rem(step, 2), lax.rem(it, 2)
+        for copy in step_copies(step, slot):
+            copy.wait()
+
+        @pl.when(step + 1 < steps)
+        def _():
+            for copy in step_copies(step + 1, 1 - slot):
+                copy.start()
+
+        @pl.when(gi == 0)
+        def _():
+            x_copy(it, x_slot).wait()
+
+            pl.when(it + 1 < tensor)(x_copy(it + 1, 1 - x_slot).start)
+            dx[...] = jnp.zeros_like(dx)
+
+            @pl.when(it + 1 == tensor)
+            def _():
+                copy = pltpu.make_async_copy(x_hbm.at[pl.ds(pl.multiple_of(p.block * rows, rows), rows)], x.at[1 - x_slot], local.at[own_sem])
+                copy.start()
+                copy.wait()
+
+        for h in range(heads):
+            cols = slice(h * 128, h * 128 + 128)
+            k = kv[slot, :, cols]
+            d = do[g, :, cols]
+            e = exps[slot, h]
+            ds = (e.astype(F32) * (dot(k, d, NT) - r[g, h:h + 1])).astype(BF16)
+            dkv[:, cols] = (dot(ds, q[g, :, cols], NN) + dot(e, d, NN)).astype(BF16)
+            dqt[g, h] += dot(k, ds, TN)
+        dk = dkv[...]
+        bias = pl.ds(8 + tensor + g, 1)
+        tiny[bias, :width] += colsum(dk)
+        dx[...] += dot(dk, w0[0, g], NT)
+        wacc[g] += dot(x[x_slot], dk, TN)
+
+        @pl.when(it == tensor - 1)
+        def _():
+            for h in range(heads):
+                cols = slice(h * 128, h * 128 + 128)
+                dq = dqt[g, h] * np.float32(HEAD ** -0.5)
+                dq = jnp.where(lax.broadcasted_iota(jnp.int32, dq.shape, 0) < HEAD, dq, 0.0)
+                dkv[:, cols] = dq.T.astype(BF16)
+            dq = dkv[...]
+            tiny[bias, width:] = colsum(dq)
+            own[...] += dot(dq, w0[1, g], NT)
+            gw[1, g] = (dot(x[1 - x_slot], dq, TN) + gw[1, g].astype(F32)).astype(BF16)
+            gw[0, g] = wacc[g].astype(BF16)
+            for f in tails:
+                f.first(tensor - 1 - gi)
+
+        @pl.when((gi == 0) & (it >= 1))
+        def _():
+            for f in folds:
+                for k in range(2, stages):
+                    f.add(k, n + 1)
+                f.line_first(n + 1)
+
+        @pl.when((gi == 0) & (it >= 2))
+        def _():
+            if p.half > 1:
+                rows_from_mate(n + 2)
+
+        @pl.when(gi == 0)
+        def _():
+            for f in folds:
+                f.add(0, n)
+
+        @pl.when((gi == min(1, tensor - 1)) & (it >= 1))
+        def _():
+            rows_from_twin(n + 1, 1 - x_slot)
+
+        @pl.when(gi == min(2, tensor - 1))
+        def _():
+            for f in folds:
+                f.add(1, n)
+
+        @pl.when((gi == tensor - 1) & (it >= 1))
+        def _():
+            for f in folds:
+                f.line_next(n + 1)
+
+        @pl.when((it == tensor - 1) & (gi >= 1))
+        def _():
+            for f in tails:
+                f.add(0, tensor - gi)
+
+        @pl.when((gi == tensor - 1) & (it < tensor - 1))
+        def _():
+            pl.when((it >= 2) & p.off)(lambda: s.left(dxb.at[x_slot], twin + p.near(n + 2)))
+            dxb[x_slot] = dx[...].astype(BF16)
+            rows_to_twin(n, x_slot)
+
+    def body(step, carry):
+        one(step // tensor, lax.rem(step, tensor))
+        return carry
+
+    lax.fori_loop(0, steps, body, 0)
+    last_slot = (tensor - 1) % 2
+
+    @pl.when(p.off)
+    def _():
+        if tensor > 2:
+            s.left(dxb.at[last_slot], twin + p.near(2))
+        dxb[last_slot] = dx[...].astype(BF16)
+        mate_in[1] = own[...].astype(BF16)
+    rows_to_twin(0, last_slot)
+    s.start(mate_in.at[1], mate_in.at[0], own_slot, p.twin, p.swap, p.off)
+
+    tiny_at = [0]
+
+    def tiny_step(begin, end):
+        k = tiny_at[0]
+        if k == len(range((fsdp * tensor).bit_length() - 1)):
+            return
+        bit = 1 << k
+        i, j = (flip(p.i, bit), p.j) if bit < fsdp else (p.i, flip(p.j, bit // fsdp))
+        copy = s.copy(tiny, tiny_in.at[k], tiny_slots + k, i, j)
+        if begin:
+            copy.start()
+        if end:
+            copy.wait_recv()
+            copy.wait_send()
+            tiny[...] += tiny_in[k]
+            tiny_at[0] += 1
+
+    tiny_step(True, False)
+    for f in folds:
+        for k in range(2, stages):
+            f.add(k, 0)
+    for f in tails:
+        f.add(0, 0)
+    for n in range(tensor)[::-1]:
+        for f in tails:
+            f.add(1, n)
+        if n < tensor - 1:
+            for f in tails:
+                for k in range(2, stages):
+                    f.add(k, n + 1)
+                f.line_first(n + 1)
+        tiny_step(False, True)
+        tiny_step(True, False)
+    for f in folds:
+        f.result()
+    for f in tails:
+        for k in range(2, stages):
+            f.add(k, 0)
+    for n in range(1, tensor)[::-1]:
+        for f in tails:
+            f.line_next(n)
+        tiny_step(False, True)
+        tiny_step(True, False)
+    while tiny_at[0] < (fsdp * tensor).bit_length() - 1:
+        tiny_step(False, True)
+        tiny_step(True, False)
+
+    @pl.when(p.on)
+    def _():
+        s.arrive(twin_in.at[p.j], twin + p.j)
+        dx[...] += own[...] + twin_in[p.j].astype(F32)
+        if p.half > 1:
+            s.arrive(mate_in.at[p.j], mate + p.j)
+            dx[...] += mate_in[p.j].astype(F32)
+
+    @pl.when(p.off)
+    def _():
+        s.arrive(fin_in, fin)
+        s.arrive(mate_in.at[0], own_slot)
+        dx[...] = fin_in[...].astype(F32) + mate_in[0].astype(F32)
+    s.arrive(swapped, swap_slot, p.off)
+    for f in tails:
+        f.result()
+    for n in range(tensor):
+        t = p.near(n)
+        if n < 2:
+            s.left(dxb.at[0], twin + t, p.off)
+        if n > 0:
+            if p.half > 1:
+                s.left(dxb.at[0], mate + t, p.on & ((n == 1) | p.is_end))
+                if n > 1:
+                    s.left(dxb.at[0], fin_send + t, p.on & p.is_edge)
+            else:
+                s.left(dxb.at[0], fin_send + t, p.on)
+    for f in folds + tails:
+        f.finish()
+    s.finish()
+
+
+def last_part(fsdp, tensor, x, w0, kv, q, do, g_o, g, e, resid, low, r, g_bup, g_vecs):
+    groups, heads, _, rows = e.shape
+    model, width = w0.shape[2:]
+    shard = model // fsdp
+    bits = fsdp.bit_length() - 1
+    vm = lambda d, *shape: pltpu.VMEM(shape, d)
+    slots = 4 * ((fsdp - 1) * tensor + 2 * tensor) + 3 * tensor + 16
+    scratch = [vm(BF16, 6, fsdp >> (k + 1), tensor, shard, width) for k in range(bits)]
+    scratch += [vm(BF16, 6, 2, tensor, shard, width), vm(BF16, 4, tensor, fsdp // 2, shard, width), vm(BF16, 2, rows, model),
+                vm(BF16, 2, tensor, model, width), vm(BF16, 2, rows, width), vm(BF16, tensor, rows, width), vm(BF16, tensor, rows, width),
+                vm(F32, tensor, heads, 128, rows), vm(F32, tensor, model, width), vm(BF16, 2, heads, rows, rows),
+                vm(BF16, 2, tensor, model, width), vm(BF16, rows, width), vm(BF16, 2, rows, model), vm(F32, rows, model), vm(BF16, tensor, rows, model),
+                vm(BF16, tensor, rows, model), vm(BF16, rows, model), vm(F32, (fsdp * tensor).bit_length() - 1, 8 + 2 * tensor, model),
+                pltpu.SemaphoreType.DMA((slots,)), pltpu.SemaphoreType.DMA((slots,)), pltpu.SemaphoreType.DMA((16 + fsdp,))]
+    return pl.pallas_call(
+        functools.partial(last_kernel, fsdp, tensor),
+        in_specs=[ANY] * 10 + [VM] * 3, out_specs=[VM] * 3 + [ANY],
+        out_shape=[jax.ShapeDtypeStruct(s, d) for s, d in [
+            ((6, shard, width), F32), ((rows, model), F32), ((8 + 2 * tensor, model), F32), ((rows, model), BF16)]],
+        scratch_shapes=scratch,
+        compiler_params=pltpu.CompilerParams(collective_id=1, has_side_effects=True, vmem_limit_bytes=65400 * 1024),
+    )(x, w0, kv, q, do, g_o, g, e, resid, low, r, g_bup, g_vecs)
 
 
 def normalize(values, gain, shift):
@@ -23,14 +961,14 @@
 
 
 def outer_sum(left, right):
-    return lax.dot_general(left, right, CONTRACT_FIRST, preferred_element_type=jnp.float32)
+    return dot(left, right, TN)
 
 
 def times_transposed(left, right):
-    return lax.dot_general(left, right, CONTRACT_LAST, preferred_element_type=jnp.float32)
-
-
-def local(
+    return dot(left, right, NT)
+
+
+def plain(
     tokens,
     cotangent,
     w_query,
@@ -272,9 +1210,69 @@
     )
 
 
+def fits(tokens, w_query, w_up):
+    fsdp, tensor = lax.axis_size("fsdp"), lax.axis_size("tensor")
+    shard, columns = w_query.shape
+    return (tensor in (2, 4) and fsdp >= 4 and fsdp & (fsdp - 1) == 0 and shard % 16 == 0 and columns >= 3 * HEAD and columns % HEAD == 0
+            and w_up.shape[1] == 4 * columns and tokens.shape[0] % 128 == 0)
+
+
+def pairs(first, second):
+    rows, columns = first.shape
+    both = jnp.stack([first.reshape(rows, -1, HEAD), second.reshape(rows, -1, HEAD)], 2)
+    return both.reshape(rows, 2 * columns)
+
+
+def layer(tokens, cotangent, w_query, w_key, w_value, w_out, w_up, w_down, b_query, b_value, b_up, b_out, b_down,
+          gain_attn, shift_attn, gain_ffn, shift_ffn):
+    if not fits(tokens, w_query, w_up):
+        return plain(tokens, cotangent, w_query, w_key, w_value, w_out, w_up, w_down, b_query, b_value, b_up, b_out, b_down,
+                     gain_attn, shift_attn, gain_ffn, shift_ffn)
+    fsdp, tensor = lax.axis_size("fsdp"), lax.axis_size("tensor")
+    i, j = lax.axis_index("fsdp"), lax.axis_index("tensor")
+    rows, model = tokens.shape
+    shard, columns = w_query.shape
+    width = 2 * columns
+    down = w_down.T
+    pack = jnp.stack([pairs(w_key, w_value), pairs(w_query, w_out.T), w_up[:, :width], down[:, :width], w_up[:, width:], down[:, width:]])
+
+    def placed(vector):
+        mine = jnp.tile(vector.astype(F32), fsdp).reshape(fsdp, -1)
+        mine = jnp.where(lax.broadcasted_iota(jnp.int32, mine.shape, 0) == i, mine, 0.0)
+        return mine.reshape(1, -1)
+
+    def spread(vector, second):
+        vector = placed(vector)
+        zero = jnp.zeros_like(vector)
+        return pairs(zero, vector) if second else pairs(vector, zero)
+
+    small = jnp.concatenate([jnp.concatenate([spread(b_value, True), spread(b_query, False)], 1), placed(b_up),
+                             *map(placed, (b_out, b_down, gain_attn, shift_attn, gain_ffn, shift_ffn))])
+    w0, w1, x, x_own, cot, kv, q, att, exps, inv, smalls = first_part(fsdp, tensor, pack, small, tokens, cotangent)
+    out, low, resid, r, do, g_o, g, g_bup, g_vecs = middle_part(x_own, cot, att, w0, w1, smalls, inv)
+    shards, grad_tokens, tiny, swapped = last_part(fsdp, tensor, x, w0, kv, q, do, g_o, g, exps, resid, low, r, g_bup, g_vecs)
+    output = jnp.where(i % 2 == j // (tensor // 2), out, swapped.astype(F32))
+
+    def apart(shard_pair):
+        both = shard_pair.reshape(shard, -1, 2, HEAD)
+        return both[:, :, 0].reshape(shard, columns), both[:, :, 1].reshape(shard, columns)
+
+    g_key, g_value = apart(shards[0])
+    g_query, g_out = apart(shards[1])
+    g_up = jnp.concatenate([shards[2], shards[4]], 1)
+    g_down = jnp.concatenate([shards[3], shards[5]], 1).T
+    mine = lambda vector, n: lax.dynamic_slice_in_dim(vector, i * n, n)
+    pick = lambda first: lax.dynamic_index_in_dim(tiny, first + j, 0, False)
+    both = pick(8 + tensor).reshape(2, -1, 2, HEAD)
+    g_bq, g_bv = both[1, :, 0].reshape(-1), both[0, :, 1].reshape(-1)
+    vectors = [mine(tiny[k], shard) for k in range(6)]
+    return (output, grad_tokens, g_query, g_key, g_value, g_out.T, g_up, g_down,
+            mine(g_bq, columns // fsdp), mine(g_bv, columns // fsdp), mine(pick(8), 2 * width // fsdp), *vectors)
+
+
 def solution(mesh):
     return jax.shard_map(
-        local,
+        layer,
         mesh=mesh,
         in_specs=(
             P(("fsdp", "tensor"), None),

time: 977 us -> 274 us (0.28)
  waiting for transfers between devices: 554 us -> 0 us
  Pallas kernels: 0 us -> 247 us
  matrix products: 186 us -> 0 us
  blocking collectives: 105 us -> 0 us
  other arithmetic: 63.6 us -> 9.16 us
  local copies, waits for them, and re-layouts: 41.2 us -> 16.4 us
  between operations: 19.5 us -> 0.91 us
    pallas_call x0 -> x3, Pallas kernels: none -> 247 us  [the longest x1 104 us: last_part(): pl.pallas_call(functools.partial(last_kernel, fsdp, tensor), in_specs=[AN...]
    reduce_scatter x6 -> x0, waiting for transfers between devices: 243 us -> none  [the longest x1 59.5 us: local(): lax.psum_scatter(jnp.dot(attended, out_weight, preferred_element_type=jnp...]
    all_gather x6 -> x0, waiting for transfers between devices: 193 us -> none  [the longest x1 63.5 us: local(): lax.all_gather(grad_resid_attn.astype(jnp.bfloat16), 'tensor', axis=0, ti...]
    dot_general x45 -> x0, matrix products: 182 us -> none  [the longest x8 34.3 us: scores_of(): jnp.einsum('qhd,khd->hqk', piece, key_heads, preferred_element_type=jnp.f...]
    unnamed x20 -> x0, waiting for transfers between devices: 118 us -> none
    unnamed x3 -> x0, blocking collectives: 68.6 us -> none
    all_gather x4 -> x0, blocking collectives: 36.5 us -> none  [the longest x1 10 us: local(): lax.all_gather(w_query, 'fsdp', axis=0, tiled=True)]
    reduce_sum x17 -> x0, other arithmetic: 28.7 us -> none  [the longest x4 9.84 us: forward_block(): total = jnp.sum(exponent, -1, keepdims=True)]
  transfers between devices with their start and end apart: 16 -> 0, of which waited for: 12 -> 0; matrix products, arithmetic and copies ran while one was open for 21% -> 0% of each run, Pallas kernels for 0% -> 0%
where the time goes in v2:
time: 274 us
  Pallas kernels  247 us (90%)
  local copies, waits for them, and re-layouts  16.4 us (6%)
  other arithmetic  9.16 us (3%)
    pallas_call x1, Pallas kernels, last_part(): pl.pallas_call(functools.partial(last_kernel, fsdp, tensor), in_specs=[AN...  104 us
    pallas_call x1, Pallas kernels, first_part(): pl.pallas_call(functools.partial(first_kernel, fsdp, tensor), in_specs=[V...  103 us
    pallas_call x1, Pallas kernels, middle_part(): pl.pallas_call(functools.partial(middle_kernel, groups), in_specs=[ANY] *...  40.4 us
    unnamed x24, local copies, waits for them, and re-layouts  6.92 us
    convert_element_type x9, other arithmetic, placed(): mine = jnp.tile(vector.astype(F32), fsdp).reshape(fsdp, -1)  5.99 us

profile of v2, /device:TPU:0, one launch (start us, length us, event | category | flops | bytes accessed | tf_op | source)
XLA Modules:
  0.0 273.7 jit_solution(9554204214825470589)
XLA Ops:
  0.7 0.7 convert_element_type.30
  1.4 0.7 convert_element_type.31
  2.5 0.7 convert_element_type.32
  3.2 0.7 convert_element_type.33
  3.8 0.7 convert_element_type.34
  4.5 0.7 convert_element_type.35
  5.2 0.7 convert_element_type.36
  5.8 0.7 convert_element_type.37
  6.5 0.7 convert_element_type.38
  7.8 0.7 concatenate.13.small
  8.4 0.9 copy.39
  9.3 0.9 copy.40
  10.4 0.9 copy.42
  11.3 0.8 pad_maximum_fusion.2
  12.5 0.8 copy-done.3
  13.2 102.8 %shard_map.296 = (bf16[2,4,768,384]{3,2,1,0:T(8,128)(2,1)}, bf16[4,4,768,384]{3,2,1,0:T(8,128)(2,1)}, bf16[2048,768]{1,0:T(8,128)(2,1)}, bf16[512,768]{1,0:T(8,1...) custom-call(bf16[6,96,384]{2,1,0:T(8,128)(2,1)} %copy-done.3, ...), custom_call_target="tpu_custom_call" | custom-call | tf_op jit(solution)/shard_map/pallas_call | solution.py:407
  116.0 40.4 %shard_map.297 = (f32[512,768]{1,0:T(8,128)}, bf16[512,768]{1,0:T(8,128)(2,1)}, f32[512,768]{1,0:T(8,128)}, f32[4,8,512]{2,1,0:T(8,128)}, bf16[4,512,384]{2,1,0:...) custom-call(bf16[512,768]{1,0:T(8,128)(2,1)} %get-tuple-element.41.x, ...), custom_call_target="tpu_custom_call" | custom-call | tf_op jit(solution)/shard_map/pallas_call | solution.py:550
  156.4 104.0 %shard_map.298 = (f32[6,96,384]{2,1,0:T(8,128)}, f32[512,768]{1,0:T(8,128)}, f32[16,768]{1,0:T(8,128)}, bf16[512,768]{1,0:T(8,128)(2,1)}) custom-call(bf16[2048,768]{1,0:T(8,128)(2,1)} %get-tuple-element.49.x_hbm, bf16[2,4,768,384]{3,2,1,0:T(8,128)(2,1)} %get-tuple-element.44.w0_hbm, bf16[4,2048,384]{2,1,0:T(8,128)(2,1)} %get-tuple-element.50.kv_hbm, ...), custom_call_target="tpu_custom_call" | custom-call | tf_op jit(solution)/shard_map/pallas_call | solution.py:942
  260.4 1.0 fusion.10
  261.5 0.6 fusion.6
  262.1 0.6 fusion.4
  262.6 0.6 fusion.2
  263.2 1.3 slice_bitcast_fusion.1
  264.5 0.9 pad_maximum_fusion
  265.4 1.3 convert_select_fusion
  266.8 0.7 fusion.8
  267.5 0.7 copy.48
  268.4 0.7 copy.49
  269.1 0.7 copy.50
  270.0 0.6 dynamic_slice.47
  271.3 1.3 dynamic-slice_bitcast_fusion
  272.5 1.1 copy.57
  (47 shorter events, 2.6 us)
Async XLA Ops:
  0.7 11.7 %copy-start.5 = (bf16[768,96]{0,1:T(8,128)(2,1)S(1)}, bf16[768,96]{0,1:T(8,128)(2,1)}, u32[]{:S(2)}) copy-start(bf16[768,96]{0,1:T(8,128)(2,1)} %param.24) | copy-start | bytes 442372
  0.7 11.7 %copy-start.4 = (bf16[96,768]{1,0:T(8,128)(2,1)S(1)}, bf16[96,768]{1,0:T(8,128)(2,1)}, u32[]{:S(2)}) copy-start(bf16[96,768]{1,0:T(8,128)(2,1)} %param.23) | copy-start | bytes 442372
  12.4 0.8 copy-start.3
  260.4 5.0 %copy-start.1 = (f32[512,768]{1,0:T(8,128)S(1)}, f32[512,768]{1,0:T(8,128)}, u32[]{:S(2)}) copy-start(f32[512,768]{1,0:T(8,128)} %get-tuple-element.48) | copy-start | bytes 4718596
  260.4 5.0 %copy-start.2 = (bf16[512,768]{1,0:T(8,128)(2,1)S(1)}, bf16[512,768]{1,0:T(8,128)(2,1)}, u32[]{:S(2)}) copy-start(bf16[512,768]{1,0:T(8,128)(2,1)} %get-tuple-element.61) | copy-start | bytes 2359300
  266.7 5.9 %copy-start = (f32[512,768]{1,0:T(8,128)S(1)}, f32[512,768]{1,0:T(8,128)}, u32[]{:S(2)}) copy-start(f32[512,768]{1,0:T(8,128)} %get-tuple-element.136) | copy-start | bytes 4718596

commit v3 on v2

--- a/solution.py
+++ b/solution.py
@@ -109,6 +109,13 @@
         return jnp.where(self.h == 0, place, self.tensor - 1 - place)
 
     def barrier(self):
+        self.greet()
+        self.met()
+
+    def met(self):
+        pl.semaphore_wait(pltpu.get_barrier_semaphore(), self.tensor + self.fsdp.bit_length() - 1)
+
+    def greet(self):
         sem = pltpu.get_barrier_semaphore()
         others = [(self.i, lax.rem(self.j + k, self.tensor)) for k in range(1, self.tensor)]
         bit = 1
@@ -118,7 +125,6 @@
         others.append((self.twin, self.swap))
         for i, j in others:
             pl.semaphore_signal(sem, inc=1, device_id=(i, j), device_id_type=MESH)
-        pl.semaphore_wait(sem, len(others))
 
 
 class Sends:
@@ -154,6 +160,47 @@
         for copy, when in self.started:
             copy.wait_send() if when is None else pl.when(when)(copy.wait_send)
         self.started = []
+
+
+def transposed(value):
+    return value.astype(F32).T.astype(value.dtype)
+
+
+def spread(lanes, n, place, first, width):
+    at = lanes(lax.broadcasted_iota(jnp.int32, (n, width), 1))
+    return jnp.where(at == lax.broadcasted_iota(jnp.int32, (n, width), 0) + place * n, 1.0, 0.0)
+
+
+def head_lanes(second):
+    def lanes(lane):
+        inside = lane % 128
+        if second:
+            return jnp.where(inside >= HEAD, lane // 128 * HEAD + inside - HEAD, -1)
+        return jnp.where(inside < HEAD, lane // 128 * HEAD + inside, -1)
+    return lanes
+
+
+def pack_own(p, w_query, w_key, w_value, w_out, w_up, w_down, vectors, pack, small):
+    shard, columns = w_query.shape
+    width = 2 * columns
+    out = transposed(w_out[...])
+    for k, (first, second) in enumerate(((w_key[...], w_value[...]), (w_query[...], out))):
+        for h in range(columns // HEAD):
+            cols = slice(h * HEAD, h * HEAD + HEAD)
+            pack[k, :, 2 * h * HEAD:2 * h * HEAD + 2 * HEAD] = jnp.concatenate([first[:, cols], second[:, cols]], 1)
+    for k in range(2):
+        cols = slice(k * width, k * width + width)
+        pack[2 + 2 * k] = w_up[:, cols]
+        pack[3 + 2 * k] = w_down[:, cols]
+    few, many = columns // p.fsdp, 2 * width // p.fsdp
+    take = lambda at, n: vectors[:, at:at + n].astype(BF16)
+    put = lambda value, ones: dot(value, ones.astype(BF16), NN)
+    small[0:1, width:] = put(take(0, few), spread(head_lanes(False), few, p.i, 0, width))
+    small[0:1, :width] = put(take(few, few), spread(head_lanes(True), few, p.i, 0, width))
+    small[1:2] = put(take(2 * few, many), spread(lambda lane: lane, many, p.i, 0, 2 * width))
+    ones = spread(lambda lane: lane, shard, p.i, 0, shard * p.fsdp)
+    for k in range(6):
+        small[2 + k:3 + k] = put(take(2 * few + many + k * shard, shard), ones)
 
 
 class Stream:
@@ -232,10 +279,12 @@
         after(h)
 
 
-def first_kernel(fsdp, tensor, pack, small, tok, cot, w0_out, w1, x_out, own_out, cot_out, kv_out, q_out, att_out, exp_out,
-                 inv, smalls, w0, sm, x, kv, q, att, s_ref, exps, send, recv, local):
+def first_kernel(fsdp, tensor, w_query, w_key, w_value, w_out, w_up, w_down, vectors, tok, cot, w0_out, w1, x_out, own_out, cot_out, kv_out, q_out, att_out, exp_out,
+                 inv, smalls, pack, small, w0, sm, x, kv, q, att, s_ref, exps, send, recv, local):
     p = Place(fsdp, tensor)
     s = Sends(p, send, recv)
+    p.greet()
+    pack_own(p, w_query, w_key, w_value, w_out, w_up, w_down, vectors, pack, small)
     rows, model = tok.shape
     shard = pack.shape[1]
     heads = exps.shape[0]
@@ -291,7 +340,7 @@
     own += [keep(pack.at[2 + k], w1.at[k, p.j, mine]) for k in range(4)]
     own += [keep(small, sm.at[p.j, pl.ds(pl.multiple_of(p.i * small.shape[0], small.shape[0]), small.shape[0])])]
     own += [keep(tok, x_at(p.j), p.on), keep(cot, cot_out, p.on)]
-    p.barrier()
+    p.met()
     for g in now:
         g.first_line()
     for g in now:
@@ -399,26 +448,104 @@
         st.finish()
 
 
-def first_part(fsdp, tensor, pack, small, tok, cot):
-    chunks, shard, width = pack.shape
+def first_part(fsdp, tensor, w_query, w_key, w_value, w_out, w_up, w_down, vectors, tok, cot):
+    shard, width = w_query.shape[0], 2 * w_query.shape[1]
     rows, model = tok.shape
     heads, keys = width // 128, tensor * rows
     slots = 5 * (tensor + 1 + (fsdp - 1) * tensor) + 8 * tensor + 1
     return pl.pallas_call(
         functools.partial(first_kernel, fsdp, tensor),
-        in_specs=[VM] * 4, out_specs=[ANY] * 9 + [VM] * 2,
+        in_specs=[VM] * 9, out_specs=[ANY] * 9 + [VM] * 2,
         out_shape=[jax.ShapeDtypeStruct(s, d) for s, d in [
             ((2, tensor, model, width), BF16), ((4, tensor, model, width), BF16), ((keys, model), BF16), ((rows, model), BF16),
             ((rows, model), BF16), ((tensor, keys, width), BF16), ((tensor, rows, width), BF16), ((tensor, rows, width), BF16),
-            ((tensor, heads, keys, rows), BF16), ((tensor, 8, rows), F32), ((tensor, *small.shape), F32)]],
+            ((tensor, heads, keys, rows), BF16), ((tensor, 8, rows), F32), ((tensor, 8, model), F32)]],
         scratch_shapes=[pltpu.VMEM(s, d) for s, d in [
-            ((2, tensor, model, width), BF16), ((tensor, fsdp * small.shape[0], model), F32), ((keys, model), BF16),
+            ((6, shard, width), BF16), ((8, model), F32),
+            ((2, tensor, model, width), BF16), ((tensor, fsdp * 8, model), F32), ((keys, model), BF16),
             ((tensor, keys, width), BF16), ((tensor, rows, width), BF16), ((tensor, rows, width), BF16), ((keys, rows), F32),
             ((heads, keys, rows), BF16)]] + [pltpu.SemaphoreType.DMA((slots,)), pltpu.SemaphoreType.DMA((slots,)),
                                              pltpu.SemaphoreType.DMA((16 + 5 * tensor + heads,))],
         compiler_params=pltpu.CompilerParams(collective_id=0, has_side_effects=True, vmem_limit_bytes=VMEM_LIMIT),
-    )(pack, small, tok, cot)
-
+    )(w_query, w_key, w_value, w_out, w_up, w_down, vectors, tok, cot)
+
+
+class Fold:
+    def __init__(self, sends, give, keep, lead, halves, inbox, order, out):
+        self.s, self.p, self.give, self.keep, self.lead = sends, sends.place, give, keep, lead
+        self.halves, self.inbox, self.order, self.out = halves, inbox, order[::-1], out
+        n = self.p.tensor
+        self.masks = [span(self.order[k + 1:]) for k in range(len(order))]
+        self.slot = [[sends.slots(n) for _ in masks] for masks in self.masks]
+        self.z = sends.slots(2 * n)
+
+    def half(self, k, mask, t):
+        return self.halves[k].at[(self.lead, self.masks[k].index(mask), t)]
+
+    def first(self, n):
+        t, bit = self.p.near(n), self.order[0]
+        for k, m in enumerate(self.masks[0]):
+            self.s.start(self.give(t, m | bit), self.half(0, m, t), self.slot[0][k] + t, flip(self.p.i, bit), self.p.j, note=False)
+
+    def add(self, k, n):
+        t = self.p.near(n)
+        for at, m in enumerate(self.masks[k]):
+            here = self.half(k, m, t)
+            self.s.arrive(here, self.slot[k][at] + t)
+            mine = self.keep(t, at) if k == 0 else self.half(k - 1, m, t)
+            here[...] = (here[...].astype(F32) + mine[...].astype(F32)).astype(BF16)
+        if k + 1 < len(self.order):
+            bit = self.order[k + 1]
+            for at, m in enumerate(self.masks[k + 1]):
+                self.s.start(self.half(k, m | bit, t), self.half(k + 1, m, t), self.slot[k + 1][at] + t,
+                             flip(self.p.i, bit), self.p.j, note=False)
+
+    def total(self, t):
+        return self.half(len(self.order) - 1, 0, t)
+
+    def way(self, n):
+        t = self.p.near(n)
+        right = t > self.p.j
+        there = self.p.j + jnp.where(right, 1, -1)
+        before = self.p.j - jnp.where(right, 1, -1)
+        side = jnp.where(right, 0, 1)
+        has = (before >= 0) & (before < self.p.tensor)
+        return t, there, has, self.inbox.at[(self.lead, side, t)], self.z + side * self.p.tensor + t
+
+    def line_first(self, n):
+        t, there, has, box, slot = self.way(n)
+        self.s.start(self.total(t), box, slot, self.p.i, there, jnp.logical_not(has), note=False)
+
+    def line_next(self, n):
+        t, there, has, box, slot = self.way(n)
+        total = self.total(t)
+
+        @pl.when(has)
+        def _():
+            self.s.arrive(box, slot)
+            box[...] = (box[...].astype(F32) + total[...].astype(F32)).astype(BF16)
+            self.s.start(box, box, slot, self.p.i, there, note=False)
+
+    def result(self):
+        p = self.p
+        self.out[...] = self.total(p.j)[...].astype(F32)
+        for side, there in ((0, p.j > 0), (1, p.j < p.tensor - 1)):
+            box = self.inbox.at[(self.lead, side, p.j)]
+
+            @pl.when(there)
+            def _(box=box, side=side):
+                self.s.arrive(box, self.z + side * p.tensor + p.j)
+                self.out[...] += box[...].astype(F32)
+
+    def finish(self):
+        here = self.half(0, self.masks[0][0], 0)
+        for n in range(self.p.tensor):
+            t = self.p.near(n)
+            for slots in self.slot:
+                for slot in slots:
+                    self.s.left(here, slot + t)
+            if n > 0:
+                self.s.left(here, self.way(n)[4])
 
 class Loads:
     def __init__(self, sems):
@@ -558,84 +685,6 @@
         + [pltpu.SemaphoreType.DMA((12 * groups + 2,))],
         compiler_params=pltpu.CompilerParams(vmem_limit_bytes=VMEM_LIMIT),
     )(x_own, cot, att, w0, w1, smalls, inv)
-
-
-class Fold:
-    def __init__(self, sends, give, keep, lead, halves, inbox, order, out):
-        self.s, self.p, self.give, self.keep, self.lead = sends, sends.place, give, keep, lead
-        self.halves, self.inbox, self.order, self.out = halves, inbox, order[::-1], out
-        n = self.p.tensor
-        self.masks = [span(self.order[k + 1:]) for k in range(len(order))]
-        self.slot = [[sends.slots(n) for _ in masks] for masks in self.masks]
-        self.z = sends.slots(2 * n)
-
-    def half(self, k, mask, t):
-        return self.halves[k].at[(self.lead, self.masks[k].index(mask), t)]
-
-    def first(self, n):
-        t, bit = self.p.near(n), self.order[0]
-        for k, m in enumerate(self.masks[0]):
-            self.s.start(self.give(t, m | bit), self.half(0, m, t), self.slot[0][k] + t, flip(self.p.i, bit), self.p.j, note=False)
-
-    def add(self, k, n):
-        t = self.p.near(n)
-        for at, m in enumerate(self.masks[k]):
-            here = self.half(k, m, t)
-            self.s.arrive(here, self.slot[k][at] + t)
-            mine = self.keep(t, at) if k == 0 else self.half(k - 1, m, t)
-            here[...] = (here[...].astype(F32) + mine[...].astype(F32)).astype(BF16)
-        if k + 1 < len(self.order):
-            bit = self.order[k + 1]
-            for at, m in enumerate(self.masks[k + 1]):
-                self.s.start(self.half(k, m | bit, t), self.half(k + 1, m, t), self.slot[k + 1][at] + t,
-                             flip(self.p.i, bit), self.p.j, note=False)
-
-    def total(self, t):
-        return self.half(len(self.order) - 1, 0, t)
-
-    def way(self, n):
-        t = self.p.near(n)
-        right = t > self.p.j
-        there = self.p.j + jnp.where(right, 1, -1)
-        before = self.p.j - jnp.where(right, 1, -1)
-        side = jnp.where(right, 0, 1)
-        has = (before >= 0) & (before < self.p.tensor)
-        return t, there, has, self.inbox.at[(self.lead, side, t)], self.z + side * self.p.tensor + t
-
-    def line_first(self, n):
-        t, there, has, box, slot = self.way(n)
-        self.s.start(self.total(t), box, slot, self.p.i, there, jnp.logical_not(has), note=False)
-
-    def line_next(self, n):
-        t, there, has, box, slot = self.way(n)
-        total = self.total(t)
-
-        @pl.when(has)
-        def _():
-            self.s.arrive(box, slot)
-            box[...] = (box[...].astype(F32) + total[...].astype(F32)).astype(BF16)
-            self.s.start(box, box, slot, self.p.i, there, note=False)
-
-    def result(self):
-        p = self.p
-        self.out[...] = self.total(p.j)[...].astype(F32)
-        for side, there in ((0, p.j > 0), (1, p.j < p.tensor - 1)):
-            box = self.inbox.at[(self.lead, side, p.j)]
-
-            @pl.when(there)
-            def _(box=box, side=side):
-                self.s.arrive(box, self.z + side * p.tensor + p.j)
-                self.out[...] += box[...].astype(F32)
-
-    def finish(self):
-        here = self.half(0, self.masks[0][0], 0)
-        for n in range(self.p.tensor):
-            t = self.p.near(n)
-            for slots in self.slot:
-                for slot in slots:
-                    self.s.left(here, slot + t)
-            if n > 0:
-                self.s.left(here, self.way(n)[4])
 
 
 def last_kernel(fsdp, tensor, x_hbm, w0_hbm, kv_hbm, q_hbm, do_hbm, g_o_hbm, g_hbm, e_hbm, resid_hbm, low_hbm, r, g_bup, g_vecs,
@@ -683,16 +732,19 @@
         copy.start()
     gets = [ld.load(do_hbm, do), ld.load(q_hbm, q)]
     x_copy(0, 0).start()
-    gets.append(ld.load(w0_hbm, w0))
+    gets.append(ld.load(w0_hbm.at[0], w0.at[0]))
+    late = [ld.load(w0_hbm.at[1], w0.at[1])]
     own_gets = [ld.load(g_hbm.at[:, :, block_rows(m)], own_g.at[:, :, at]) for at, m in enumerate(stay)]
-    gets.append(ld.load(g_o_hbm, gw.at[1]))
-    gets.append(ld.load(resid_hbm, own))
+    late += [ld.load(g_o_hbm, gw.at[1]), ld.load(resid_hbm, own)]
     own_sem = ld.slots(1)
     tiny[:8] = g_vecs[...]
     for t in range(tensor):
         tiny[8 + t:9 + t] = g_bup[t]
     tiny[8 + tensor:] = jnp.zeros_like(tiny[8 + tensor:])
-    p.barrier()
+    p.greet()
+    wacc[...] = jnp.zeros_like(wacc)
+    dqt[...] = jnp.zeros_like(dqt)
+    p.met()
     for n in range(tensor)[::-1]:
         for f in folds:
             f.first(n)
@@ -701,9 +753,7 @@
     twin, mate, fin = s.slots(tensor), s.slots(tensor), s.slots(1)
     fin_send, own_slot = s.slots(tensor), s.slots(1)
     tiny_slots = s.slots((fsdp * tensor).bit_length() - 1)
-    wacc[...] = jnp.zeros_like(wacc)
-    dqt[...] = jnp.zeros_like(dqt)
-    for copy in gets + own_gets:
+    for copy in gets:
         copy.wait()
 
     def rows_to_twin(n, slot):
@@ -787,6 +837,11 @@
             gw[0, g] = wacc[g].astype(BF16)
             for f in tails:
                 f.first(tensor - 1 - gi)
+
+        @pl.when(step == 0)
+        def _():
+            for copy in own_gets + late:
+                copy.wait()
 
         @pl.when((gi == 0) & (it >= 1))
         def _():
@@ -947,6 +1002,62 @@
         scratch_shapes=scratch,
         compiler_params=pltpu.CompilerParams(collective_id=1, has_side_effects=True, vmem_limit_bytes=65400 * 1024),
     )(x, w0, kv, q, do, g_o, g, e, resid, low, r, g_bup, g_vecs)
+
+
+def final_kernel(fsdp, tensor, shards, dx, tiny, out, swapped,
+                 output, grad_tokens, g_query, g_key, g_value, g_out, g_up, g_down, b_query, b_value, b_up, *vectors):
+    p = Place(fsdp, tensor)
+    columns, width = g_query.shape[1], shards.shape[2]
+    shard = shards.shape[1]
+    grad_tokens[...] = dx[...]
+
+    @pl.when(p.on)
+    def _():
+        output[...] = out[...]
+
+    @pl.when(p.off)
+    def _():
+        output[...] = swapped[...].astype(F32)
+    heads = [(h, slice(h * HEAD, h * HEAD + HEAD), slice(2 * h * HEAD, 2 * h * HEAD + 2 * HEAD)) for h in range(columns // HEAD)]
+    out_rows = []
+    for h, cols, both in heads:
+        keys, query = shards[0, :, both], shards[1, :, both]
+        g_key[:, cols], g_value[:, cols] = keys[:, :HEAD], keys[:, HEAD:]
+        g_query[:, cols] = query[:, :HEAD]
+        out_rows.append(query[:, HEAD:])
+    g_out[...] = jnp.concatenate(out_rows, 1).T
+    for k in range(2):
+        cols = slice(k * width, k * width + width)
+        g_up[:, cols] = shards[2 + 2 * k]
+        g_down[:, cols] = shards[3 + 2 * k]
+
+    def take(row, ones):
+        return lax.dot_general(row, ones, ((NT[:1], NT[1:]), ((), ())), precision=lax.Precision.HIGHEST, preferred_element_type=F32)
+
+    few, many = columns // fsdp, 2 * width // fsdp
+    both = tiny[pl.ds(8 + tensor + p.j, 1), :]
+    b_query[...] = take(both[:, width:], spread(head_lanes(False), few, p.i, 0, width))
+    b_value[...] = take(both[:, :width], spread(head_lanes(True), few, p.i, 0, width))
+    b_up[...] = take(tiny[pl.ds(8 + p.j, 1), :], spread(lambda lane: lane, many, p.i, 0, 2 * width))
+    rows = take(tiny[:8], spread(lambda lane: lane, shard, p.i, 0, shard * fsdp))
+    for k, vector in enumerate(vectors):
+        vector[...] = rows[k:k + 1]
+
+
+def final_part(fsdp, tensor, shards, dx, tiny, out, swapped):
+    _, shard, width = shards.shape
+    rows, model = dx.shape
+    columns = width // 2
+    flat, square = (rows, model), (shard, columns)
+    results = pl.pallas_call(
+        functools.partial(final_kernel, fsdp, tensor),
+        in_specs=[VM] * 5, out_specs=[VM] * 17,
+        out_shape=[jax.ShapeDtypeStruct(s, F32) for s in [
+            flat, flat, square, square, square, (columns, shard), (shard, 2 * width), (shard, 2 * width),
+            (1, columns // fsdp), (1, columns // fsdp), (1, 2 * width // fsdp)] + [(1, shard)] * 6],
+        compiler_params=pltpu.CompilerParams(vmem_limit_bytes=VMEM_LIMIT),
+    )(shards, dx, tiny, out, swapped)
+    return (*results[:7], results[7].T, *[r.reshape(-1) for r in results[8:]])
 
 
 def normalize(values, gain, shift):
@@ -1213,14 +1324,8 @@
 def fits(tokens, w_query, w_up):
     fsdp, tensor = lax.axis_size("fsdp"), lax.axis_size("tensor")
     shard, columns = w_query.shape
-    return (tensor in (2, 4) and fsdp >= 4 and fsdp & (fsdp - 1) == 0 and shard % 16 == 0 and columns >= 3 * HEAD and columns % HEAD == 0
+    return (tensor == 4 and fsdp >= 4 and fsdp & (fsdp - 1) == 0 and shard % 16 == 0 and 4 * columns == tokens.shape[1] and columns >= 3 * HEAD and columns % HEAD == 0
             and w_up.shape[1] == 4 * columns and tokens.shape[0] % 128 == 0)
-
-
-def pairs(first, second):
-    rows, columns = first.shape
-    both = jnp.stack([first.reshape(rows, -1, HEAD), second.reshape(rows, -1, HEAD)], 2)
-    return both.reshape(rows, 2 * columns)
 
 
 def layer(tokens, cotangent, w_query, w_key, w_value, w_out, w_up, w_down, b_query, b_value, b_up, b_out, b_down,
@@ -1229,45 +1334,16 @@
         return plain(tokens, cotangent, w_query, w_key, w_value, w_out, w_up, w_down, b_query, b_value, b_up, b_out, b_down,
                      gain_attn, shift_attn, gain_ffn, shift_ffn)
     fsdp, tensor = lax.axis_size("fsdp"), lax.axis_size("tensor")
-    i, j = lax.axis_index("fsdp"), lax.axis_index("tensor")
-    rows, model = tokens.shape
-    shard, columns = w_query.shape
-    width = 2 * columns
-    down = w_down.T
-    pack = jnp.stack([pairs(w_key, w_value), pairs(w_query, w_out.T), w_up[:, :width], down[:, :width], w_up[:, width:], down[:, width:]])
-
-    def placed(vector):
-        mine = jnp.tile(vector.astype(F32), fsdp).reshape(fsdp, -1)
-        mine = jnp.where(lax.broadcasted_iota(jnp.int32, mine.shape, 0) == i, mine, 0.0)
-        return mine.reshape(1, -1)
-
-    def spread(vector, second):
-        vector = placed(vector)
-        zero = jnp.zeros_like(vector)
-        return pairs(zero, vector) if second else pairs(vector, zero)
-
-    small = jnp.concatenate([jnp.concatenate([spread(b_value, True), spread(b_query, False)], 1), placed(b_up),
-                             *map(placed, (b_out, b_down, gain_attn, shift_attn, gain_ffn, shift_ffn))])
-    w0, w1, x, x_own, cot, kv, q, att, exps, inv, smalls = first_part(fsdp, tensor, pack, small, tokens, cotangent)
+    pieces = (b_query, b_value, b_up, b_out, b_down, gain_attn, shift_attn, gain_ffn, shift_ffn)
+    total, at, vectors = sum(piece.size for piece in pieces), 0, 0.0
+    for piece in pieces:
+        vectors += jnp.pad(piece.reshape(1, -1), ((0, 0), (at, total - at - piece.size)))
+        at += piece.size
+    w0, w1, x, x_own, cot, kv, q, att, exps, inv, smalls = first_part(
+        fsdp, tensor, w_query, w_key, w_value, w_out, w_up, w_down.T, vectors, tokens, cotangent)
     out, low, resid, r, do, g_o, g, g_bup, g_vecs = middle_part(x_own, cot, att, w0, w1, smalls, inv)
     shards, grad_tokens, tiny, swapped = last_part(fsdp, tensor, x, w0, kv, q, do, g_o, g, exps, resid, low, r, g_bup, g_vecs)
-    output = jnp.where(i % 2 == j // (tensor // 2), out, swapped.astype(F32))
-
-    def apart(shard_pair):
-        both = shard_pair.reshape(shard, -1, 2, HEAD)
-        return both[:, :, 0].reshape(shard, columns), both[:, :, 1].reshape(shard, columns)
-
-    g_key, g_value = apart(shards[0])
-    g_query, g_out = apart(shards[1])
-    g_up = jnp.concatenate([shards[2], shards[4]], 1)
-    g_down = jnp.concatenate([shards[3], shards[5]], 1).T
-    mine = lambda vector, n: lax.dynamic_slice_in_dim(vector, i * n, n)
-    pick = lambda first: lax.dynamic_index_in_dim(tiny, first + j, 0, False)
-    both = pick(8 + tensor).reshape(2, -1, 2, HEAD)
-    g_bq, g_bv = both[1, :, 0].reshape(-1), both[0, :, 1].reshape(-1)
-    vectors = [mine(tiny[k], shard) for k in range(6)]
-    return (output, grad_tokens, g_query, g_key, g_value, g_out.T, g_up, g_down,
-            mine(g_bq, columns // fsdp), mine(g_bv, columns // fsdp), mine(pick(8), 2 * width // fsdp), *vectors)
+    return final_part(fsdp, tensor, shards, grad_tokens, tiny, out, swapped)
 
 
 def solution(mesh):

time: 274 us -> 251 us (0.916)
  local copies, waits for them, and re-layouts: 16.4 us -> 0 us
  other arithmetic: 9.16 us -> 1.45 us
    unnamed x24 -> x0, local copies, waits for them, and re-layouts: 6.92 us -> none
    convert_element_type x9 -> x0, other arithmetic: 5.99 us -> none  [placed(): mine = jnp.tile(vector.astype(F32), fsdp).reshape(fsdp, -1)]
    pallas_call x0 -> x1, Pallas kernels: none -> 4.6 us  [final_part(): pl.pallas_call(functools.partial(final_kernel, fsdp, tensor), in_specs=[V...]
    dynamic_slice x6 -> x0, local copies, waits for them, and re-layouts: 4.21 us -> none  [layer(): mine = lambda vector, n: lax.dynamic_slice_in_dim(vector, i * n, n)]
    pallas_call x1, Pallas kernels: 104 us -> 101 us  [last_part(): pl.pallas_call(functools.partial(last_kernel, fsdp, tensor), in_specs=[AN...]
where the time goes in v3:
time: 251 us
  Pallas kernels  249 us (99%)
    pallas_call x1, Pallas kernels, first_part(): pl.pallas_call(functools.partial(first_kernel, fsdp, tensor), in_specs=[V...  102 us
    pallas_call x1, Pallas kernels, last_part(): pl.pallas_call(functools.partial(last_kernel, fsdp, tensor), in_specs=[AN...  101 us
    pallas_call x1, Pallas kernels, middle_part(): pl.pallas_call(functools.partial(middle_kernel, groups), in_specs=[ANY] *...  40.3 us

profile of v3, /device:TPU:0, one launch (start us, length us, event | category | flops | bytes accessed | tf_op | source)
XLA Modules:
  0.0 250.9 jit_solution(924351352445920863)
XLA Ops:
  0.7 1.5 pad_add_fusion.vectors
  2.1 102.5 %shard_map.296 = (bf16[2,4,768,384]{3,2,1,0:T(8,128)(2,1)}, bf16[4,4,768,384]{3,2,1,0:T(8,128)(2,1)}, bf16[2048,768]{1,0:T(8,128)(2,1)}, bf16[512,768]{1,0:T(8,1...) custom-call(bf16[96,192]{1,0:T(8,128)(2,1)} %w_query.1, ...), custom_call_target="tpu_custom_call" | custom-call | tf_op jit(solution)/shard_map/pallas_call | solution.py:456
  104.6 40.3 %shard_map.297 = (f32[512,768]{1,0:T(8,128)}, bf16[512,768]{1,0:T(8,128)(2,1)}, f32[512,768]{1,0:T(8,128)}, f32[4,8,512]{2,1,0:T(8,128)}, bf16[4,512,384]{2,1,0:...) custom-call(bf16[512,768]{1,0:T(8,128)(2,1)} %get-tuple-element.62.x, ...), custom_call_target="tpu_custom_call" | custom-call | tf_op jit(solution)/shard_map/pallas_call | solution.py:677
  144.9 101.2 %shard_map.298 = (f32[6,96,384]{2,1,0:T(8,128)}, f32[512,768]{1,0:T(8,128)}, f32[16,768]{1,0:T(8,128)}, bf16[512,768]{1,0:T(8,128)(2,1)}) custom-call(bf16[2048,768]{1,0:T(8,128)(2,1)} %get-tuple-element.58.x_hbm, bf16[2,4,768,384]{3,2,1,0:T(8,128)(2,1)} %get-tuple-element.59.w0_hbm, bf16[4,2048,384]{2,1,0:T(8,128)(2,1)} %get-tuple-element.60.kv_hbm, ...), custom_call_target="tpu_custom_call" | custom-call | tf_op jit(solution)/shard_map/pallas_call | solution.py:997
  246.1 4.6 %shard_map.299 = (f32[512,768]{1,0:T(8,128)}, f32[512,768]{1,0:T(8,128)}, f32[96,192]{1,0:T(8,128)}, f32[96,192]{1,0:T(8,128)}, f32[96,192]{1,0:T(8,128)}, /*ind...) custom-call(f32[6,96,384]{2,1,0:T(8,128)} %get-tuple-element.77.shar, ...), custom_call_target="tpu_custom_call" | custom-call | tf_op jit(solution)/shard_map/pallas_call | solution.py:1052

commit v4 on v3

--- a/solution.py
+++ b/solution.py
@@ -603,9 +603,9 @@
     acc[...] = hidden + vec(1)
 
     def forward(g, c):
+        for get in gets:
+            get(g)
         for k in range(2):
-            gets[2 * k](g)
-            gets[2 * k + 1](g)
             pre = dot(hl[...], w1[2 * k, g], NN) + smalls[g, 1:2, k * width:(k + 1) * width]
             phi = 0.5 + 0.5 * lax.erf(pre * np.float32(0.5 ** 0.5))
             slope[g, k] = phi + pre * (jnp.exp(-0.5 * pre * pre) * np.float32((2 * np.pi) ** -0.5))
@@ -630,13 +630,13 @@
     def back(g, c):
         for k in range(2):
             grads[2 * k + 1, g] = dot(low[...], act[g, k], TN).astype(BF16)
-            put(2 * k + 1, g).start()
             gp = (dot(low[...], w1[2 * k + 1, g], NN) * slope[g, k]).astype(BF16)
             act[g, k] = gp
             g_bup[g, :, k * width:(k + 1) * width] = colsum(gp)
             grads[2 * k, g] = dot(hl[...], gp, TN).astype(BF16)
-            put(2 * k, g).start()
             acc[...] += dot(act[g, k], w1[2 * k, g], NT)
+        for k in range(4):
+            put(k, g).start()
         return c
 
     lax.fori_loop(0, groups, back, 0)
@@ -658,8 +658,8 @@
             scale = inv[g, h:h + 1]
             r_ref[g, h:h + 1] = jnp.sum(prod[cols], axis=0, keepdims=True) * scale
             datt[g, :, cols] = (da[cols] * scale).T.astype(BF16)
+        g_o[g] = dot(low[...], att[g], TN).astype(BF16)
         put(4, g).start()
-        g_o[g] = dot(low[...], att[g], TN).astype(BF16)
         put(5, g).start()
         return c
 

time: 251 us -> 250 us (level)
  no operation moved by 1% of the time
where the time goes in v4:
time: 250 us
  Pallas kernels  247 us (99%)
    pallas_call x1, Pallas kernels, first_part(): pl.pallas_call(functools.partial(first_kernel, fsdp, tensor), in_specs=[V...  102 us
    pallas_call x1, Pallas kernels, last_part(): pl.pallas_call(functools.partial(last_kernel, fsdp, tensor), in_specs=[AN...  101 us
    pallas_call x1, Pallas kernels, middle_part(): pl.pallas_call(functools.partial(middle_kernel, groups), in_specs=[ANY] *...  39 us

profile of v4, /device:TPU:0, one launch (start us, length us, event | category | flops | bytes accessed | tf_op | source)
XLA Modules:
  0.0 249.5 jit_solution(8235410960445617406)
XLA Ops:
  0.7 1.5 pad_add_fusion.vectors
  2.1 102.5 %shard_map.296 = (bf16[2,4,768,384]{3,2,1,0:T(8,128)(2,1)}, bf16[4,4,768,384]{3,2,1,0:T(8,128)(2,1)}, bf16[2048,768]{1,0:T(8,128)(2,1)}, bf16[512,768]{1,0:T(8,1...) custom-call(bf16[96,192]{1,0:T(8,128)(2,1)} %w_query.1, ...), custom_call_target="tpu_custom_call" | custom-call | tf_op jit(solution)/shard_map/pallas_call | solution.py:456
  104.6 39.0 %shard_map.297 = (f32[512,768]{1,0:T(8,128)}, bf16[512,768]{1,0:T(8,128)(2,1)}, f32[512,768]{1,0:T(8,128)}, f32[4,8,512]{2,1,0:T(8,128)}, bf16[4,512,384]{2,1,0:...) custom-call(bf16[512,768]{1,0:T(8,128)(2,1)} %get-tuple-element.62.x, ...), custom_call_target="tpu_custom_call" | custom-call | tf_op jit(solution)/shard_map/pallas_call | solution.py:677
  143.5 101.2 %shard_map.298 = (f32[6,96,384]{2,1,0:T(8,128)}, f32[512,768]{1,0:T(8,128)}, f32[16,768]{1,0:T(8,128)}, bf16[512,768]{1,0:T(8,128)(2,1)}) custom-call(bf16[2048,768]{1,0:T(8,128)(2,1)} %get-tuple-element.58.x_hbm, bf16[2,4,768,384]{3,2,1,0:T(8,128)(2,1)} %get-tuple-element.59.w0_hbm, bf16[4,2048,384]{2,1,0:T(8,128)(2,1)} %get-tuple-element.60.kv_hbm, ...), custom_call_target="tpu_custom_call" | custom-call | tf_op jit(solution)/shard_map/pallas_call | solution.py:997
  244.7 4.6 %shard_map.299 = (f32[512,768]{1,0:T(8,128)}, f32[512,768]{1,0:T(8,128)}, f32[96,192]{1,0:T(8,128)}, f32[96,192]{1,0:T(8,128)}, f32[96,192]{1,0:T(8,128)}, /*ind...) custom-call(f32[6,96,384]{2,1,0:T(8,128)} %get-tuple-element.77.shar, ...), custom_call_target="tpu_custom_call" | custom-call | tf_op jit(solution)/shard_map/pallas_call | solution.py:1052

commit v5 on v4

--- a/solution.py
+++ b/solution.py
@@ -864,7 +864,7 @@
         def _():
             rows_from_twin(n + 1, 1 - x_slot)
 
-        @pl.when(gi == min(2, tensor - 1))
+        @pl.when(gi == tensor - 1)
         def _():
             for f in folds:
                 f.add(1, n)

time: 250 us -> 249 us (level)
  no operation moved by 1% of the time
where the time goes in v5:
time: 249 us
  Pallas kernels  247 us (99%)
    pallas_call x1, Pallas kernels, first_part(): pl.pallas_call(functools.partial(first_kernel, fsdp, tensor), in_specs=[V...  102 us
    pallas_call x1, Pallas kernels, last_part(): pl.pallas_call(functools.partial(last_kernel, fsdp, tensor), in_specs=[AN...  101 us
    pallas_call x1, Pallas kernels, middle_part(): pl.pallas_call(functools.partial(middle_kernel, groups), in_specs=[ANY] *...  39 us

profile of v5, /device:TPU:0, one launch (start us, length us, event | category | flops | bytes accessed | tf_op | source)
XLA Modules:
  0.0 248.9 jit_solution(3924330788719081149)
XLA Ops:
  0.7 1.5 pad_add_fusion.vectors
  2.1 102.5 %shard_map.296 = (bf16[2,4,768,384]{3,2,1,0:T(8,128)(2,1)}, bf16[4,4,768,384]{3,2,1,0:T(8,128)(2,1)}, bf16[2048,768]{1,0:T(8,128)(2,1)}, bf16[512,768]{1,0:T(8,1...) custom-call(bf16[96,192]{1,0:T(8,128)(2,1)} %w_query.1, ...), custom_call_target="tpu_custom_call" | custom-call | tf_op jit(solution)/shard_map/pallas_call | solution.py:456
  104.6 39.0 %shard_map.297 = (f32[512,768]{1,0:T(8,128)}, bf16[512,768]{1,0:T(8,128)(2,1)}, f32[512,768]{1,0:T(8,128)}, f32[4,8,512]{2,1,0:T(8,128)}, bf16[4,512,384]{2,1,0:...) custom-call(bf16[512,768]{1,0:T(8,128)(2,1)} %get-tuple-element.62.x, ...), custom_call_target="tpu_custom_call" | custom-call | tf_op jit(solution)/shard_map/pallas_call | solution.py:677
  143.5 100.6 %shard_map.298 = (f32[6,96,384]{2,1,0:T(8,128)}, f32[512,768]{1,0:T(8,128)}, f32[16,768]{1,0:T(8,128)}, bf16[512,768]{1,0:T(8,128)(2,1)}) custom-call(bf16[2048,768]{1,0:T(8,128)(2,1)} %get-tuple-element.58.x_hbm, bf16[2,4,768,384]{3,2,1,0:T(8,128)(2,1)} %get-tuple-element.59.w0_hbm, bf16[4,2048,384]{2,1,0:T(8,128)(2,1)} %get-tuple-element.60.kv_hbm, ...), custom_call_target="tpu_custom_call" | custom-call | tf_op jit(solution)/shard_map/pallas_call | solution.py:997
  244.2 4.6 %shard_map.299 = (f32[512,768]{1,0:T(8,128)}, f32[512,768]{1,0:T(8,128)}, f32[96,192]{1,0:T(8,128)}, f32[96,192]{1,0:T(8,128)}, f32[96,192]{1,0:T(8,128)}, /*ind...) custom-call(f32[6,96,384]{2,1,0:T(8,128)} %get-tuple-element.77.shar, ...), custom_call_target="tpu_custom_call" | custom-call | tf_op jit(solution)/shard_map/pallas_call | solution.py:1052
